TPU v7x, 512 devices: a whole 4x8x8 slice. The times are simulated.
512 devices in a mesh: row: 16 (over z, core), ma: 32 (over x, y).
Axes of the slice: x: 4, y: 8, z: 8, core: 2. Of those that a mesh axis runs over, the one named last changes fastest.
Arguments:
- toroidal_stream_spectra: float32 [2, 16, 512, 512], P(None, 'row', 'ma'), may hold values from -6 to 6, as said below
- thermal_spectra: float32 [2, 16, 512, 512], P(None, 'row', 'ma'), may hold values from -6 to 6, as said below
- induction_potential: float32 [2, 16, 512, 512], P(None, 'row', 'ma'), may hold values from -6 to 6, as said below
- outward_speed_spectra: float32 [2, 16, 512, 512], P(None, 'row', 'ma'), may hold values from -60 to 60, as said below
- position_azimuth_map: int32 [512], replicated, may hold values from 0 to 511, as said below
- subdiagonal_complement: float32 [2, 16, 512], P(None, 'row'), may hold values from 0.005 to 0.3
- superdiagonal_complement: float32 [2, 16, 512], P(None, 'row'), may hold values from 0.005 to 0.3
- diagonal_entries: float32 [2, 16, 512], P(None, 'row'), may hold values from 2 to 16
Outputs:
- new_temperature: float32 [2, 16, 512, 512], P(None, 'row', 'ma')
- new_magnetic: float32 [2, 16, 512, 512], P(None, 'row', 'ma')
Inputs may be any that keep to these rules, and one draw needn't show every extreme that they name: `position_azimuth_map`: slots 2 i and 2 i + 1 hold the orders m and 511 - m; every order stands in exactly one slot. `toroidal_stream_spectra`: an entry whose degree is below the order of its slot in position_azimuth_map is zero. `thermal_spectra`: an entry whose degree is below the order of its slot in position_azimuth_map is zero. `induction_potential`: an entry whose degree is below the order of its slot in position_azimuth_map is zero. `outward_speed_spectra`: an entry whose degree is below the order of its slot in position_azimuth_map is zero.
All inputs are finite; a program needn't handle non-finite values.
Results may differ from a plain program's by a relative error of at most 0.00035.
Values sent between devices are 32-bit elements; how exact they have to be, the bound alone decides.
No kernel may reach another device: no remote copies, remote signals or barrier semaphores. Data moves between devices by JAX's collectives and lax.ppermute only.
A program may use at most 128 MiB of HBM per device.

v0:
```python
import math

import jax
import jax.numpy as jnp
import numpy as np
from jax import lax
from jax.experimental import pallas as pl
from jax.experimental.pallas import tpu as pltpu
from jax.sharding import PartitionSpec as P

NLAT = 768
NLON = 1536
NORTH = NLAT // 2
DEG = 512
QUARTER = NLON // 4
GROUP = 16
SHELLS = 16
INNER = 0.35
SPAN = 0.65
STEP = 0.001
RENORM = 32
INTERPRET = False

f32 = jnp.float32
bf16 = jnp.bfloat16
i32 = jnp.int32


def host_tables():
    theta = np.pi * (np.arange(NORTH) + 0.5) / NLAT
    lat = np.zeros((8, NORTH), np.float32)
    lat[0] = np.cos(theta)
    lat[1] = np.log(np.sin(theta))
    orders = np.arange(DEG)
    log_norm = np.array(
        [
            0.5 * (math.lgamma(m + 1.5) - math.lgamma(m + 1.0) - math.lgamma(1.5))
            - 0.5 * math.log(2.0)
            for m in orders
        ]
    )
    norm = np.zeros((8, DEG), np.float32)
    norm[0] = log_norm
    k = np.arange(1, NLAT // 2 + 1)
    weights = (
        2.0
        / NLAT
        * (1.0 - 2.0 * np.sum(np.cos(2.0 * k[:, None] * theta[None]) / (4.0 * k * k - 1.0)[:, None], 0))
    )
    plain = -np.concatenate([weights, weights]) / NLON
    scaled = plain / np.concatenate([np.sin(theta), np.sin(theta)]) ** 2
    per = np.stack([scaled, plain]).reshape(2, 3, 32, 8).transpose(2, 0, 1, 3).reshape(32, 2, 24)
    return lat, norm, per.astype(np.float32)


def split(x):
    high = x.astype(bf16)
    return high, (x - high.astype(f32)).astype(bf16)


def dot_nn(a, b):
    return lax.dot_general(a, b, (((1,), (0,)), ((), ())), preferred_element_type=f32)


def dot_nt(a, b):
    return lax.dot_general(a, b, (((1,), (1,)), ((), ())), preferred_element_type=f32)


def roll_lanes(x, shift):
    return pltpu.roll(x, shift % x.shape[1], 1)


def block_swap(arrays, width):
    arrays = list(arrays)
    count = len(arrays)
    lane = lax.broadcasted_iota(i32, arrays[0].shape, 1) // width
    bit = 1
    while bit < count:
        low = (lane & bit) == 0
        fresh = list(arrays)
        for a in range(count):
            if a & bit == 0:
                b = a | bit
                fresh[a] = jnp.where(low, arrays[a], roll_lanes(arrays[b], bit * width))
                fresh[b] = jnp.where(low, roll_lanes(arrays[a], -bit * width), arrays[b])
        arrays = fresh
        bit *= 2
    return arrays


def pair_slot(map_ref, first, place):
    par = place // 8
    pair = place % 8
    odd = lax.rem(map_ref[first + 2 * pair], 2)
    return 2 * pair + lax.rem(odd + par, 2)


def synthesis_kernel(
    place_ref, map_ref, psi_ref, temp_ref, mag_ref, speed_ref, low_ref, high_ref, lat_ref, norm_ref,
    chunk_ref, high_tab_ref, low_tab_ref, table, coefs, rows,
):
    step = pl.program_id(0)
    first = place_ref[0] * GROUP

    @pl.when(step == 0)
    def _():
        row16 = lax.broadcasted_iota(i32, (GROUP, 128), 0)
        natural = jnp.zeros((GROUP, 128), f32)
        ordered = jnp.zeros((GROUP, 128), f32)
        for s in range(GROUP):
            natural = jnp.where(row16 == s, map_ref[first + s].astype(f32), natural)
            slot = pair_slot(map_ref, first, s)
            ordered = jnp.where(row16 == s, map_ref[first + slot].astype(f32), ordered)
        m = natural[:, :1]
        degree = lax.broadcasted_iota(i32, (GROUP, DEG), 1).astype(f32)
        above = degree > m
        link = jnp.where(
            above,
            jnp.sqrt(
                jnp.maximum((2.0 * degree + 1.0) * (degree * degree - m * m), 0.0)
                / jnp.maximum(2.0 * degree - 1.0, 1.0)
            ),
            0.0,
        )
        weight = jnp.where(m == 0.0, 1.0, 2.0)

        def keep(at, value):
            for t in range(4):
                coefs[t, at * GROUP : (at + 1) * GROUP, :] = value[:, t * 128 : (t + 1) * 128]

        inverse = 1.0 / (2.0 * (SPAN / SHELLS))
        for q, ref in enumerate((psi_ref, temp_ref, mag_ref)):
            for c in range(2):
                value = ref[c * GROUP : (c + 1) * GROUP, :] * weight
                turned = m * value if c == 0 else -m * value
                keep(2 * q + (1 - c), turned)
                keep(6 + 2 * q + c, value * degree)
                keep(12 + 2 * q + c, roll_lanes(value * link, -1))
        for c in range(2):
            part = slice(c * GROUP, (c + 1) * GROUP)
            keep(18 + c, speed_ref[part, :] * weight)
            for q in range(2):
                slope = (high_ref[q, part, :] - low_ref[q, part, :]) * inverse
                keep(20 + 2 * q + c, slope * weight)
        m = ordered[:, :1]
        above = degree > m
        square = degree * degree - m * m
        denominator = jnp.where(above, square, 1.0)
        rise = jnp.where(
            above, jnp.sqrt(jnp.maximum(4.0 * degree * degree - 1.0, 1.0) / denominator), 0.0
        )
        lower = (degree - 1.0) * (degree - 1.0) - m * m
        fall = jnp.where(
            above,
            jnp.sqrt(
                jnp.maximum((2.0 * degree + 1.0) * lower, 0.0)
                / (jnp.maximum(2.0 * degree - 3.0, 1.0) * denominator)
            ),
            0.0,
        )
        log_norm = jnp.sum(jnp.where(degree == m, norm_ref[0:1, :], 0.0), axis=1, keepdims=True)
        x = jnp.broadcast_to(lat_ref[0:1, :], (GROUP, NORTH))
        log_scale = log_norm + m * lat_ref[1:2, :]
        before = jnp.zeros((GROUP, NORTH), f32)
        current = jnp.zeros((GROUP, NORTH), f32)
        order = ordered[:, :1]
        for tile in range(DEG // RENORM):
            scale = jnp.exp(log_scale)
            for l in range(tile * RENORM, (tile + 1) * RENORM):
                fresh = rise[:, l : l + 1] * x * current - fall[:, l : l + 1] * before
                fresh = jnp.where(order == float(l), 1.0, fresh)
                before, current = current, fresh
                value = fresh * scale
                for t in range(3):
                    table[t, l * GROUP : (l + 1) * GROUP, :] = value[:, t * 128 : (t + 1) * 128]
            magnitude = jnp.maximum(jnp.abs(before), jnp.abs(current))
            magnitude = jnp.where(magnitude > 0.0, magnitude, 1.0)
            inverse_magnitude = 1.0 / magnitude
            before = before * inverse_magnitude
            current = current * inverse_magnitude
            log_scale = log_scale + jnp.log(magnitude)

    legendre = jnp.concatenate(
        [table[t, pl.ds(step, DEG, stride=GROUP), :] for t in range(3)], axis=1
    )
    leg_high, leg_low = split(legendre)
    high_tab_ref[0] = leg_high
    low_tab_ref[0] = leg_low

    slot = pair_slot(map_ref, first, step)
    par = step // 8
    north = jnp.concatenate(
        [coefs[t, pl.ds(slot, 24, stride=GROUP), :] for t in range(4)], axis=1
    )
    degree = lax.broadcasted_iota(i32, (24, DEG), 1)
    south = jnp.where(lax.rem(degree + par, 2) == 0, north, -north)
    north_high, north_low = split(north)
    south_high, south_low = split(south)
    high = jnp.concatenate([north_high, south_high], axis=0)
    both = jnp.concatenate([high, north_low, south_low], axis=0)
    first_part = dot_nn(both, leg_high)
    result = first_part[:48] + (first_part[48:] + dot_nn(high, leg_low))
    x = lat_ref[0:1, :]
    base = par * 16 + lax.rem(step, 8)
    for hemi in range(2):
        r = result[24 * hemi : 24 * hemi + 24]
        slant = (x if hemi == 0 else -x) * r[6:12] - r[12:18]
        for q in range(9):
            for c in range(2):
                at = 2 * q + c
                if q < 3:
                    line = r[at : at + 1]
                elif q < 6:
                    line = slant[at - 6 : at - 5]
                else:
                    line = r[at + 6 : at + 7]
                rows[hemi, pl.ds(q * 32 + base + 8 * c, 1), :] = line

    @pl.when(step == GROUP - 1)
    def _():
        for tile in range(2):
            turned = [
                jnp.transpose(rows[h, tile * 128 : (tile + 1) * 128, :]) for h in range(2)
            ]
            turned = jnp.concatenate(turned, axis=0)
            for blk in range(3):
                at = tile * 24 + blk * 8
                chunk_ref[:, at : at + 8, :] = turned[blk * 256 : (blk + 1) * 256].reshape(32, 8, 128)
        rest = jnp.concatenate([rows[0, 256:288, :], rows[1, 256:288, :]], axis=1)
        rest = jnp.concatenate(
            [rest[:, b * 256 : (b + 1) * 256] for b in range(3)] + [jnp.zeros((32, 256), f32)], axis=0
        )
        chunk_ref[:, 48:56, :] = jnp.transpose(rest).reshape(32, 8, 128)


def synthesis(place, orders, psi, temp, mag, speed, low, high, lat, norm):
    whole = lambda *shape: pl.BlockSpec(shape, lambda i: (0,) * len(shape))
    smem = pl.BlockSpec(memory_space=pltpu.SMEM)
    return pl.pallas_call(
        synthesis_kernel,
        grid=(GROUP,),
        in_specs=[smem, smem] + [whole(32, DEG)] * 4 + [whole(2, 32, DEG)] * 2
        + [whole(8, NORTH), whole(8, DEG)],
        out_specs=[
            whole(32, 56, 128),
            pl.BlockSpec((1, DEG, NORTH), lambda i: (i, 0, 0)),
            pl.BlockSpec((1, DEG, NORTH), lambda i: (i, 0, 0)),
        ],
        out_shape=[
            jax.ShapeDtypeStruct((32, 56, 128), f32),
            jax.ShapeDtypeStruct((GROUP, DEG, NORTH), bf16),
            jax.ShapeDtypeStruct((GROUP, DEG, NORTH), bf16),
        ],
        scratch_shapes=[
            pltpu.VMEM((3, DEG * GROUP, 128), f32),
            pltpu.VMEM((4, 24 * GROUP, 128), f32),
            pltpu.VMEM((2, 288, NORTH), f32),
        ],
        interpret=INTERPRET,
        name="synthesis",
    )(place, orders, psi, temp, mag, speed, low, high, lat, norm)


def grid_kernel(x_ref, wave_ref, factor_ref, out_ref, stage):
    for half in range(2):
        lanes = slice(half * 128, (half + 1) * 128)
        for tile in range(2):
            got = block_swap(
                [x_ref[half * 16 + s, tile * 24 : tile * 24 + 24, :] for s in range(16)], 8
            )
            for g in range(16):
                q = tile * 4 + g // 4
                stage[g % 4, q * 24 : (q + 1) * 24, lanes] = got[g]
        got = block_swap([x_ref[half * 16 + s, 48:56, :] for s in range(16)], 8)
        for g in range(12):
            at = 8 * 24 + (g // 4) * 8
            stage[g % 4, at : at + 8, lanes] = got[g]
    tables = [split(wave_ref[pc]) for pc in range(4)]
    waves = []
    for pc in range(4):
        high, low = split(stage[pc])
        wave_high, wave_low = tables[pc]
        waves.append(dot_nn(high, wave_high) + (dot_nn(low, wave_high) + dot_nn(high, wave_low)))
    cos_even, sin_even, cos_odd, sin_odd = waves
    ce, se = cos_even + cos_odd, sin_even + sin_odd
    co, so = cos_even - cos_odd, sin_even - sin_odd
    images = [ce + se, ce - se, co - so, co + so]
    f1 = factor_ref[0:24, :]
    f2 = factor_ref[24:48, :]
    f1 = jnp.concatenate([f1] * 3, axis=1)
    f2 = jnp.concatenate([f2] * 3, axis=1)
    forced = []
    for g in images:
        part = [g[q * 24 : (q + 1) * 24] for q in range(9)]
        heat = (part[3] * part[1] - part[0] * part[4]) * f1 + part[6] * part[7] * f2
        field = (part[3] * part[2] - part[0] * part[5]) * f1 + part[6] * part[8] * f2
        forced.append(jnp.concatenate([heat, field], axis=0))
    a, b = forced[0] + forced[1], forced[2] + forced[3]
    d, e = forced[0] - forced[1], forced[3] - forced[2]
    sides = [a + b, d + e, a - b, d - e]
    for par in range(2):
        parts = []
        for c in range(2):
            pc = par * 2 + c
            high, low = split(sides[pc])
            wave_high, wave_low = tables[pc]
            parts.append(dot_nt(wave_high, high) + (dot_nt(wave_high, low) + dot_nt(wave_low, high)))
        both = jnp.concatenate(parts + [jnp.zeros((256, 32), f32)], axis=1)
        out_ref[:, par * 8 : par * 8 + 8, :] = both.reshape(32, 8, 128)


def grid_stage(x, wave, factor):
    return pl.pallas_call(
        grid_kernel,
        out_shape=jax.ShapeDtypeStruct((32, 16, 128), f32),
        scratch_shapes=[pltpu.VMEM((4, 216, 256), f32)],
        interpret=INTERPRET,
        name="forcing",
    )(x, wave, factor)


def analysis_kernel(
    place_ref, map_ref, v_ref, temp_ref, mag_ref, radial_ref, high_tab_ref, low_tab_ref, out_ref, sums, right
):
    step = pl.program_id(0)
    first = place_ref[0] * GROUP

    @pl.when(step == 0)
    def _():
        for par in range(2):
            halves = [
                block_swap(
                    [v_ref[half * 16 + s, par * 8 : par * 8 + 8, :] for s in range(16)], 8
                )
                for half in range(2)
            ]
            for c in range(2):
                for f in range(2):
                    tiles = []
                    for blk in range(3):
                        g = c * 6 + f * 3 + blk
                        tiles += [halves[0][g], halves[1][g]]
                    for eo in range(2):
                        at = par * 64 + (eo * 4 + f * 2 + c) * 8
                        for t in range(3):
                            mixed = tiles[t] + tiles[t + 3] if eo == 0 else tiles[t] - tiles[t + 3]
                            sums[t, at : at + 8, :] = mixed

    par = step // 8
    slot = pair_slot(map_ref, first, step)
    start = par * 64 + lax.rem(step, 8)
    value = jnp.concatenate(
        [sums[t, pl.ds(start, 8, stride=8), :] for t in range(3)], axis=1
    )
    high, low = split(value)
    leg_high = high_tab_ref[0]
    leg_low = low_tab_ref[0]
    first_part = dot_nt(jnp.concatenate([high, low], axis=0), leg_high)
    result = first_part[:8] + (first_part[8:] + dot_nt(high, leg_low))
    degree = lax.broadcasted_iota(i32, (4, DEG), 1)
    tendency = jnp.where(lax.rem(degree + par, 2) == 0, result[:4], result[4:])
    for fc in range(4):
        right[fc, pl.ds(slot, 1), :] = tendency[fc : fc + 1]

    @pl.when(step == GROUP - 1)
    def _():
        for fc in range(4):
            f, c = fc // 2, fc % 2
            base = temp_ref if f == 0 else mag_ref
            right[fc, 0:GROUP, :] = base[c * GROUP : (c + 1) * GROUP, :] + STEP * right[fc, 0:GROUP, :]
            right[fc, GROUP : GROUP + 8, :] = radial_ref[f]
        for tile in range(4):
            got = block_swap([right[fc, :, tile * 128 : (tile + 1) * 128] for fc in range(4)], 32)
            for r in range(4):
                out_ref[tile * 4 + r] = got[r]


def analysis(place, orders, v, temp, mag, radial, high_tab, low_tab):
    whole = lambda *shape: pl.BlockSpec(shape, lambda i: (0,) * len(shape))
    smem = pl.BlockSpec(memory_space=pltpu.SMEM)
    return pl.pallas_call(
        analysis_kernel,
        grid=(GROUP,),
        in_specs=[smem, smem, whole(32, 16, 128), whole(32, DEG), whole(32, DEG), whole(2, 8, DEG),
                  pl.BlockSpec((1, DEG, NORTH), lambda i: (i, 0, 0)),
                  pl.BlockSpec((1, DEG, NORTH), lambda i: (i, 0, 0))],
        out_specs=whole(16, 24, 128),
        out_shape=jax.ShapeDtypeStruct((16, 24, 128), f32),
        scratch_shapes=[pltpu.VMEM((3, 128, 128), f32), pltpu.VMEM((4, GROUP + 8, DEG), f32)],
        interpret=INTERPRET,
        name="analysis",
    )(place, orders, v, temp, mag, radial, high_tab, low_tab)


def solve_kernel(x_ref, out_ref):
    running = jnp.zeros((GROUP, 128), f32)
    scaled = []
    for k in range(SHELLS):
        running = x_ref[k, 0:GROUP, :] + (1.0 - x_ref[k, GROUP : GROUP + 1, :]) * running
        scaled.append(running / x_ref[k, GROUP + 1 : GROUP + 2, :])
    running = jnp.zeros((GROUP, 128), f32)
    for k in reversed(range(SHELLS)):
        running = scaled[k] + (1.0 - x_ref[k, GROUP + 2 : GROUP + 3, :]) * running
        out_ref[k] = running


def solve(x):
    return pl.pallas_call(
        solve_kernel,
        out_shape=jax.ShapeDtypeStruct((SHELLS, GROUP, 128), f32),
        interpret=INTERPRET,
        name="radial",
    )(x)


def gather_kernel(x_ref, temp_ref, mag_ref):
    for tile in range(4):
        got = block_swap([x_ref[tile * 4 + r] for r in range(4)], 32)
        lanes = slice(tile * 128, (tile + 1) * 128)
        for fc in range(4):
            ref = temp_ref if fc < 2 else mag_ref
            c = fc % 2
            ref[c * GROUP : (c + 1) * GROUP, lanes] = got[fc]


def gather_stage(x):
    return pl.pallas_call(
        gather_kernel,
        out_shape=[jax.ShapeDtypeStruct((32, DEG), f32)] * 2,
        interpret=INTERPRET,
        name="assemble",
    )(x)


def wave_tables(orders):
    pair = orders.reshape(DEG // 2, 2)
    swap = pair[:, :1] % 2 == 1
    pair = jnp.where(swap, pair[:, ::-1], pair)
    node = 2 * jnp.arange(QUARTER, dtype=i32) + 1
    tables = []
    for par in range(2):
        phase = pair[:, par][:, None] * node[None, :] % (2 * NLON)
        angle = math.pi / NLON * phase.astype(f32)
        tables += [jnp.cos(angle), -jnp.sin(angle)]
    return jnp.stack(tables)


def factors(lat_place, shell, per):
    spacing = SPAN / SHELLS
    radius = INNER + spacing * (shell.astype(f32) + 0.5)
    mine = lax.dynamic_index_in_dim(jnp.asarray(per), lat_place, 0, False)
    rows = jnp.concatenate([mine[0] / (radius * radius), mine[1]])
    return jnp.broadcast_to(rows[:, None], (48, 128))


def body(
    toroidal_stream_spectra,
    thermal_spectra,
    induction_potential,
    outward_speed_spectra,
    position_azimuth_map,
    subdiagonal_complement,
    superdiagonal_complement,
    diagonal_entries,
):
    lat, norm, per = host_tables()
    place = lax.axis_index("ma")
    shell = lax.axis_index("row")
    place_array = place.reshape(1).astype(i32)
    flat = lambda a: a.reshape(32, DEG)
    psi, temp, mag, speed = map(
        flat,
        (toroidal_stream_spectra, thermal_spectra, induction_potential, outward_speed_spectra),
    )
    coupled = jnp.stack([temp, mag])
    forward = [(i, i + 1) for i in range(SHELLS - 1)]
    low = lax.ppermute(coupled, "row", forward)
    high = lax.ppermute(coupled, "row", [(b, a) for a, b in forward])
    chunk, high_tab, low_tab = synthesis(
        place_array, position_azimuth_map, psi, temp, mag, speed, low, high, jnp.asarray(lat), jnp.asarray(norm)
    )
    chunk = lax.all_to_all(chunk, "ma", 0, 0, tiled=True)
    spectra = grid_stage(chunk, wave_tables(position_azimuth_map), factors(place, shell, per))
    spectra = lax.all_to_all(spectra, "ma", 0, 0, tiled=True)
    radial = jnp.concatenate(
        [subdiagonal_complement, diagonal_entries, superdiagonal_complement, jnp.zeros((2, 5, DEG), f32)],
        axis=1,
    )
    right = analysis(place_array, position_azimuth_map, spectra, temp, mag, radial, high_tab, low_tab)
    right = lax.all_to_all(right, "row", 0, 0, tiled=True)
    solved = lax.all_to_all(solve(right), "row", 0, 0, tiled=True)
    new_temp, new_mag = gather_stage(solved)
    shape = thermal_spectra.shape
    return new_temp.reshape(shape), new_mag.reshape(shape)


def solution(mesh):
    spectra = P(None, "row", "ma", None)
    radial = P(None, "row", None)
    in_specs = (spectra,) * 4 + (P(),) + (radial,) * 3
    return jax.shard_map(
        body, mesh=mesh, in_specs=in_specs, out_specs=(spectra, spectra), check_vma=False
    )
```

profile of v0, /device:TPU:1, one launch (start us, length us, event | category | flops | bytes accessed | tf_op | source)
XLA Modules:
  0.0 142.9 jit_solution(3149697870520320289)
XLA Ops:
  0.6 0.0 copy-start.4
  0.6 0.9 pad_maximum_fusion.1
  1.5 5.4 %collective-permute-start = (f32[2,32,512]{2,1,0:T(8,128)S(1)}, f32[2,32,512]{2,1,0:T(8,128)S(1)}, u32[]{:S(2)}, u32[]{:S(2)}) collective-permute-start(f32[2,32,512]{2,1,0:T(8,128)S(1)} %pad_maximum_fusion.1), channel_id=1, source_target_pairs={{0,32},{32,64},{64,96},{96,128},{128,160},{160,192},{192,224},{224... | collective-permute-start | bytes 393224 | tf_op jit(solution)/shard_map/ppermute | solution.py:477
  6.9 4.7 %collective-permute-start.1 = (f32[2,32,512]{2,1,0:T(8,128)S(1)}, f32[2,32,512]{2,1,0:T(8,128)S(1)}, u32[]{:S(2)}, u32[]{:S(2)}) collective-permute-start(f32[2,32,512]{2,1,0:T(8,128)S(1)} %pad_maximum_fusion.1), channel_id=1, source_target_pairs={{32,0},{64,32},{96,64},{128,96},{160,128},{192,160},{224,192},{256... | collective-permute-start | bytes 393224 | tf_op jit(solution)/shard_map/ppermute | solution.py:478
  11.6 0.0 collective-permute-done.low_ref
  11.6 0.0 copy-start.2
  11.6 1.6 %collective-permute-done.1.high_ref = f32[2,32,512]{2,1,0:T(8,128)S(1)} collective-permute-done((f32[2,32,512]{2,1,0:T(8,128)S(1)}, f32[2,32,512]{2,1,0:T(8,128)S(1)}, u32[]{:S(2)}, u32[]{:S(2)}) %collective-permute-start.1) | collective-permute-done | bytes 131104 | tf_op jit(solution)/shard_map/ppermute | solution.py:478
  13.2 0.0 copy-start.3
  13.2 0.0 copy-done.2
  13.2 0.6 copy-done.3
  13.9 19.3 %synthesis.1 = (f32[32,56,128]{2,1,0:T(8,128)}, bf16[16,512,384]{2,1,0:T(8,128)(2,1)}, bf16[16,512,384]{2,1,0:T(8,128)(2,1)}) custom-call(s32[1]{0:T(128)} %bitcast.place_ref, s32[512]{0:T(512)} %map_ref.3, f32[32,512]{1,0:T(8,128)} %bitcast.23, f32[32,512]{1,0:T(8,128)} %bitcast.18, f32[32,512]{1,0:T(8,128)} %bitcast.21, f32[32,512]{1,0:T(8,128)} %bitcast.24, ...), custom_call_target="tpu_custom_call" | custom-call | tf_op jit(solution)/shard_map/synthesis/pallas_call | solution.py:239
  33.2 9.6 %all-to-all-start = ((f32[32,56,128]{2,1,0:T(8,128)}), f32[32,56,128]{2,1,0:T(8,128)S(1)}, u32[]{:S(2)}, u32[]{:S(2)}) async-start(f32[32,56,128]{2,1,0:T(8,128)} %get-tuple-element.7), calls=%async_computation | async-start | bytes 1835008 | tf_op jit(solution)/shard_map/all_to_all | solution.py:482
  42.8 0.0 copy-done.4
  42.8 0.1 reshape.313
  43.0 0.2 rev.3
  43.2 0.7 constant_dynamic-slice_fusion
  43.9 0.1 pad_maximum_fusion.2
  44.0 0.1 fusion.14
  44.1 0.1 broadcast_select_fusion
  44.2 0.2 slice_reduce_fusion.1
  44.4 3.3 %fusion.9 = (f32[1,256,384]{2,1,0:T(8,128)S(1)}, f32[1,256,384]{2,1,0:T(8,128)S(1)}, f32[1,256,384]{2,1,0:T(8,128)S(1)}, f32[1,256,384]{2,1,0:T(8,128)S(1)}) fusion(s32[384]{0:T(512)S(1)} %multiply_add_fusion, s32[256]{0:T(256)S(1)} %get-tuple-element.16, s32[256]{0:T(256)S(1)} %get-tuple-element.17), kind=kLoop, calls=%fused_computation.16 | loop fusion | flops 1966080 | bytes 1576448 | tf_op jit(solution)/shard_map/cos | solution.py:444
  47.7 1.3 pad_maximum_fusion.wave_ref
  49.0 17.9 %all-to-all-done.x_ref = f32[32,56,128]{2,1,0:T(8,128)S(1)} async-done(((f32[32,56,128]{2,1,0:T(8,128)}), f32[32,56,128]{2,1,0:T(8,128)S(1)}, u32[]{:S(2)}, u32[]{:S(2)}) %all-to-all-start) | async-done | bytes 917536 | tf_op jit(solution)/shard_map/all_to_all | solution.py:482
  66.9 0.0 copy-start
  66.9 0.8 broadcast_in_dim.23.factor_ref
  67.7 0.2 copy-done
  67.8 0.0 copy-start.5
  67.8 0.0 copy-start.6
  67.8 0.0 copy-start.7
  67.8 4.9 %forcing.1 = f32[32,16,128]{2,1,0:T(8,128)} custom-call(f32[32,56,128]{2,1,0:T(8,128)} %copy-done, f32[4,256,384]{2,1,0:T(8,128)} %pad_maximum_fusion.wave_ref, f32[48,128]{1,0:T(8,128)} %broadcast_in_dim.23.factor_ref), custom_call_target="tpu_custom_call" | custom-call | tf_op jit(solution)/shard_map/forcing/pallas_call | solution.py:313
  72.8 4.5 %all-to-all-start.1 = ((f32[32,16,128]{2,1,0:T(8,128)}), f32[32,16,128]{2,1,0:T(8,128)S(1)}, u32[]{:S(2)}, u32[]{:S(2)}) async-start(f32[32,16,128]{2,1,0:T(8,128)} %forcing.1), calls=%async_computation.1 | async-start | bytes 524288 | tf_op jit(solution)/shard_map/all_to_all | solution.py:484
  77.3 0.1 pad.3.clone
  77.4 0.0 copy-done.5
  77.4 0.0 copy-done.6
  77.4 0.0 copy-done.7
  77.4 0.7 maximum_maximum_fusion.radial_ref
  78.1 10.2 %all-to-all-done.1.v_ref = f32[32,16,128]{2,1,0:T(8,128)S(1)} async-done(((f32[32,16,128]{2,1,0:T(8,128)}), f32[32,16,128]{2,1,0:T(8,128)S(1)}, u32[]{:S(2)}, u32[]{:S(2)}) %all-to-all-start.1) | async-done | bytes 262176 | tf_op jit(solution)/shard_map/all_to_all | solution.py:484
  88.3 0.0 copy-start.1
  88.3 0.7 copy-done.1
  89.0 13.9 %analysis.1 = f32[16,24,128]{2,1,0:T(8,128)} custom-call(s32[1]{0:T(128)} %bitcast.place_ref, s32[512]{0:T(512)} %map_ref.3, f32[32,16,128]{2,1,0:T(8,128)} %copy-done.1, f32[32,512]{1,0:T(8,128)} %bitcast.19, f32[32,512]{1,0:T(8,128)} %bitcast.22, f32[2,8,512]{2,1,0:T(8,128)} %maximum_maximum_fusion.radial_ref, ...), custom_call_target="tpu_custom_call" | custom-call | tf_op jit(solution)/shard_map/analysis/pallas_call | solution.py:381
  102.9 24.0 %all_to_all.20.x_ref = f32[16,24,128]{2,1,0:T(8,128)} all-to-all(f32[16,24,128]{2,1,0:T(8,128)} %analysis.1), channel_id=1, replica_groups=mesh['row'=16,'ma'=32] {'row'}, dimensions={0} | all-to-all | bytes 393216 | tf_op jit(solution)/shard_map/all_to_all | solution.py:490
  126.9 1.6 %radial.1 = f32[16,16,128]{2,1,0:T(8,128)} custom-call(f32[16,24,128]{2,1,0:T(8,128)} %all_to_all.20.x_ref), custom_call_target="tpu_custom_call" | custom-call | tf_op jit(solution)/shard_map/radial/pallas_call | solution.py:408
  128.6 12.6 %all_to_all.21.x_ref = f32[16,16,128]{2,1,0:T(8,128)} all-to-all(f32[16,16,128]{2,1,0:T(8,128)} %radial.1), channel_id=1, replica_groups=mesh['row'=16,'ma'=32] {'row'}, dimensions={0} | all-to-all | bytes 262144 | tf_op jit(solution)/shard_map/all_to_all | solution.py:491
  141.2 1.7 %assemble.1 = (f32[32,512]{1,0:T(8,128)}, f32[32,512]{1,0:T(8,128)}) custom-call(f32[16,16,128]{2,1,0:T(8,128)} %all_to_all.21.x_ref), custom_call_target="tpu_custom_call" | custom-call | tf_op jit(solution)/shard_map/assemble/pallas_call | solution.py:427
  (3 shorter events, 0.0 us)
Async XLA Ops:
  0.6 42.2 %copy-start.4 = (s32[512]{0:T(512)S(1)}, s32[512]{0:T(512)}, u32[]{:S(2)}) copy-start(s32[512]{0:T(512)} %map_ref.3) | copy-start | bytes 6148
  1.5 10.1 %collective-permute-start = (f32[2,32,512]{2,1,0:T(8,128)S(1)}, f32[2,32,512]{2,1,0:T(8,128)S(1)}, u32[]{:S(2)}, u32[]{:S(2)}) collective-permute-start(f32[2,32,512]{2,1,0:T(8,128)S(1)} %pad_maximum_fusion.1), channel_id=1, source_target_pairs={{0,32},{32,64},{64,96},{96,128},{128,160},{160,192},{192,224},{224... | collective-permute-start | bytes 393224 | tf_op jit(solution)/shard_map/ppermute | solution.py:477
  6.9 6.3 %collective-permute-start.1 = (f32[2,32,512]{2,1,0:T(8,128)S(1)}, f32[2,32,512]{2,1,0:T(8,128)S(1)}, u32[]{:S(2)}, u32[]{:S(2)}) collective-permute-start(f32[2,32,512]{2,1,0:T(8,128)S(1)} %pad_maximum_fusion.1), channel_id=1, source_target_pairs={{32,0},{64,32},{96,64},{128,96},{160,128},{192,160},{224,192},{256... | collective-permute-start | bytes 393224 | tf_op jit(solution)/shard_map/ppermute | solution.py:478
  11.6 1.6 %copy-start.2 = (f32[2,32,512]{2,1,0:T(8,128)}, f32[2,32,512]{2,1,0:T(8,128)S(1)}, u32[]{:S(2)}) copy-start(f32[2,32,512]{2,1,0:T(8,128)S(1)} %collective-permute-done.low_ref) | copy-start | bytes 393220
  13.2 0.6 copy-start.3
  33.2 33.7 %all-to-all-start = ((f32[32,56,128]{2,1,0:T(8,128)}), f32[32,56,128]{2,1,0:T(8,128)S(1)}, u32[]{:S(2)}, u32[]{:S(2)}) async-start(f32[32,56,128]{2,1,0:T(8,128)} %get-tuple-element.7), calls=%async_computation | async-start | bytes 1835008 | tf_op jit(solution)/shard_map/all_to_all | solution.py:482
  66.9 0.9 copy-start
  67.8 9.6 %copy-start.5 = (f32[2,1,512]{2,1,0:T(1,128)S(1)}, f32[2,1,512]{2,1,0:T(1,128)}, u32[]{:S(2)}) copy-start(f32[2,1,512]{2,1,0:T(1,128)} %param.17) | copy-start | bytes 12292
  67.8 9.6 %copy-start.6 = (f32[2,1,512]{2,1,0:T(1,128)S(1)}, f32[2,1,512]{2,1,0:T(1,128)}, u32[]{:S(2)}) copy-start(f32[2,1,512]{2,1,0:T(1,128)} %param.18) | copy-start | bytes 12292
  67.8 9.6 %copy-start.7 = (f32[2,1,512]{2,1,0:T(1,128)S(1)}, f32[2,1,512]{2,1,0:T(1,128)}, u32[]{:S(2)}) copy-start(f32[2,1,512]{2,1,0:T(1,128)} %param.16) | copy-start | bytes 12292
  72.8 15.6 %all-to-all-start.1 = ((f32[32,16,128]{2,1,0:T(8,128)}), f32[32,16,128]{2,1,0:T(8,128)S(1)}, u32[]{:S(2)}, u32[]{:S(2)}) async-start(f32[32,16,128]{2,1,0:T(8,128)} %forcing.1), calls=%async_computation.1 | async-start | bytes 524288 | tf_op jit(solution)/shard_map/all_to_all | solution.py:484
  88.3 0.7 copy-start.1
where the time goes:
time: 144 us; the launch traced here: 143 us
  Pallas kernels  41.5 us (29%)
  blocking collectives  36.7 us (25%)
  waiting for transfers between devices  29.8 us (21%)
  starting transfers between devices  24.2 us (17%)
  other arithmetic  6.45 us (4%)
  local copies, waits for them, and re-layouts  3.6 us (2%)
    all_to_all x1, blocking collectives, body(): right = lax.all_to_all(right, 'row', 0, 0, tiled=True)  24 us
    pallas_call x1, Pallas kernels, synthesis(): pl.pallas_call(synthesis_kernel, grid=(GROUP,), in_specs=[smem, smem] + [...  19.3 us
    all_to_all x1, waiting for transfers between devices, body(): chunk = lax.all_to_all(chunk, 'ma', 0, 0, tiled=True)  17.9 us
    pallas_call x1, Pallas kernels, analysis(): pl.pallas_call(analysis_kernel, grid=(GROUP,), in_specs=[smem, smem, whol...  13.9 us
    all_to_all x1, blocking collectives, body(): solved = lax.all_to_all(solve(right), 'row', 0, 0, tiled=True)  12.6 us
    all_to_all x1, waiting for transfers between devices, body(): spectra = lax.all_to_all(spectra, 'ma', 0, 0, tiled=True)  10.2 us
    all_to_all x1, starting transfers between devices, body(): chunk = lax.all_to_all(chunk, 'ma', 0, 0, tiled=True)  9.64 us
    ppermute x1, starting transfers between devices, body(): low = lax.ppermute(coupled, 'row', forward)  5.38 us
  transfers between devices with their start and end apart: 4, of which 3 were waited for; matrix products, arithmetic and copies ran while one was open for 5% of the time, Pallas kernels for 0%

commit v1 on v0

v1 whole, which is shorter than its diff:
```python
import math

import jax
import jax.numpy as jnp
import numpy as np
from jax import lax
from jax.experimental import pallas as pl
from jax.experimental.pallas import tpu as pltpu
from jax.sharding import PartitionSpec as P

NLAT = 768
NLON = 1536
NORTH = NLAT // 2
DEG = 512
QUARTER = NLON // 4
GROUP = 16
PAIRS = GROUP // 2
UNROLL = 4
SHELLS = 16
INNER = 0.35
SPAN = 0.65
STEP = 0.001
RENORM = 32
INTERPRET = False
ITEMS = [(q, blk) for blk in range(3) for q in (1, 2)] + [
    (q, blk) for q in (0, 3, 4, 5, 6) for blk in range(3)
]

f32 = jnp.float32
bf16 = jnp.bfloat16
i32 = jnp.int32


def host_tables():
    theta = np.pi * (np.arange(NORTH) + 0.5) / NLAT
    lat = np.zeros((8, NORTH), np.float32)
    lat[0] = np.cos(theta)
    lat[1] = np.log(np.sin(theta))
    orders = np.arange(DEG)
    log_norm = np.array(
        [
            0.5 * (math.lgamma(m + 1.5) - math.lgamma(m + 1.0) - math.lgamma(1.5))
            - 0.5 * math.log(2.0)
            for m in orders
        ]
    )
    norm = np.zeros((8, DEG), np.float32)
    norm[0] = log_norm
    k = np.arange(1, NLAT // 2 + 1)
    weights = (
        2.0
        / NLAT
        * (1.0 - 2.0 * np.sum(np.cos(2.0 * k[:, None] * theta[None]) / (4.0 * k * k - 1.0)[:, None], 0))
    )
    plain = -np.concatenate([weights, weights]) / NLON
    scaled = plain / np.concatenate([np.sin(theta), np.sin(theta)]) ** 2
    per = np.zeros((48, 128), np.float32)
    per[:, :32] = np.stack([scaled, plain]).reshape(2, 3, 32, 8).transpose(0, 1, 3, 2).reshape(48, 32)
    return lat, norm, per


def split(x):
    high = x.astype(bf16)
    return high, (x - high.astype(f32)).astype(bf16)


def dot_nn(a, b):
    return lax.dot_general(a, b, (((1,), (0,)), ((), ())), preferred_element_type=f32)


def dot_nt(a, b):
    return lax.dot_general(a, b, (((1,), (1,)), ((), ())), preferred_element_type=f32)


def roll_lanes(x, shift):
    return pltpu.roll(x, shift % x.shape[1], 1)


def block_swap(arrays, width):
    arrays = list(arrays)
    count = len(arrays)
    lane = lax.broadcasted_iota(i32, arrays[0].shape, 1) // width
    bit = 1
    while bit < count:
        low = (lane & bit) == 0
        fresh = list(arrays)
        for a in range(count):
            if a & bit == 0:
                b = a | bit
                fresh[a] = jnp.where(low, arrays[a], roll_lanes(arrays[b], bit * width))
                fresh[b] = jnp.where(low, roll_lanes(arrays[a], -bit * width), arrays[b])
        arrays = fresh
        bit *= 2
    return arrays


def pair_orders(map_ref, first, pair):
    one = map_ref[first + 2 * pair]
    two = map_ref[first + 2 * pair + 1]
    swap = (one > two).astype(i32)
    return 2 * pair + swap, 2 * pair + 1 - swap, jnp.minimum(one, two)


def legendre_table(map_ref, first, lat_ref, norm_ref, table, last):
    row8 = lax.broadcasted_iota(i32, (PAIRS, 128), 0)
    smaller = jnp.zeros((PAIRS, 128), f32)
    for i in range(PAIRS):
        smaller = jnp.where(row8 == i, pair_orders(map_ref, first, i)[2].astype(f32), smaller)
    small = smaller[:, :1]
    place = lax.broadcasted_iota(i32, (PAIRS, DEG + 128), 1).astype(f32)
    front = place <= small
    m = jnp.where(front, DEG - 1.0 - small, small)
    degree = jnp.where(front, DEG - 1.0 - small + place, place - 1.0)
    above = degree > m
    square = degree * degree - m * m
    denominator = jnp.where(above, square, 1.0)
    rise = jnp.where(
        above, jnp.sqrt(jnp.maximum(4.0 * degree * degree - 1.0, 1.0) / denominator), 0.0
    )
    lower = (degree - 1.0) * (degree - 1.0) - m * m
    fall = jnp.where(
        above,
        jnp.sqrt(
            jnp.maximum((2.0 * degree + 1.0) * lower, 0.0)
            / (jnp.maximum(2.0 * degree - 3.0, 1.0) * denominator)
        ),
        0.0,
    )
    wide = lax.broadcasted_iota(i32, (PAIRS, DEG), 1).astype(f32)

    def start(order):
        log_norm = jnp.sum(jnp.where(wide == order, norm_ref[0:1, :], 0.0), axis=1, keepdims=True)
        return log_norm + order * lat_ref[1:2, :]

    x = jnp.broadcast_to(lat_ref[0:1, :], (PAIRS, NORTH))
    log_scale = start(DEG - 1.0 - small)
    log_small = start(small)
    scale_small = jnp.exp(log_small)
    seed = small + 1.0
    before = jnp.zeros((PAIRS, NORTH), f32)
    current = jnp.ones((PAIRS, NORTH), f32)
    for tile in range(DEG // RENORM + 1):
        scale = jnp.exp(log_scale)
        for p in range(tile * RENORM, min((tile + 1) * RENORM, DEG + 1)):
            if p > 0:
                fresh = rise[:, p : p + 1] * x * current - fall[:, p : p + 1] * before
                seeded = seed == float(p)
                fresh = jnp.where(seeded, 1.0, fresh)
                scale = jnp.where(seeded, scale_small, scale)
                before, current = current, fresh
            value = current * scale
            if p < DEG:
                for t in range(3):
                    table[t, p * PAIRS : (p + 1) * PAIRS, :] = value[:, t * 128 : (t + 1) * 128]
            else:
                last[...] = value
        magnitude = jnp.maximum(jnp.abs(before), jnp.abs(current))
        magnitude = jnp.where(magnitude > 0.0, magnitude, 1.0)
        inverse_magnitude = 1.0 / magnitude
        before = before * inverse_magnitude
        current = current * inverse_magnitude
        here = (seed >= float(tile * RENORM)) & (seed < float((tile + 1) * RENORM))
        log_scale = jnp.where(here, log_small, log_scale) + jnp.log(magnitude)


def pair_tile(table, pair, half, t):
    start = half * (DEG // 2) * PAIRS + pair
    high, low = split(table[t, pl.ds(start, DEG // 2, stride=PAIRS), :])
    return jnp.concatenate([high, low], axis=1)


def synthesis_kernel(
    place_ref, map_ref, psi_ref, temp_ref, mag_ref, speed_ref, lat_ref, norm_ref,
    chunk_ref, table, last, coefs, rows,
):
    first = place_ref[0] * GROUP
    legendre_table(map_ref, first, lat_ref, norm_ref, table, last)

    def prepare():
        row16 = lax.broadcasted_iota(i32, (GROUP, 128), 0)
        natural = jnp.zeros((GROUP, 128), f32)
        for s in range(GROUP):
            natural = jnp.where(row16 == s, map_ref[first + s].astype(f32), natural)
        m = natural[:, :1]
        degree = lax.broadcasted_iota(i32, (GROUP, DEG), 1).astype(f32)
        link = jnp.where(
            degree > m,
            jnp.sqrt(
                jnp.maximum((2.0 * degree + 1.0) * (degree * degree - m * m), 0.0)
                / jnp.maximum(2.0 * degree - 1.0, 1.0)
            ),
            0.0,
        )
        weight = jnp.where(m == 0.0, 1.0, 2.0)

        def keep(at, value):
            for t in range(4):
                coefs[t, at * GROUP : (at + 1) * GROUP, :] = value[:, t * 128 : (t + 1) * 128]

        for q, ref in enumerate((psi_ref, temp_ref, mag_ref)):
            for c in range(2):
                value = ref[c * GROUP : (c + 1) * GROUP, :] * weight
                if q == 0:
                    keep(1 - c, m * value if c == 0 else -m * value)
                else:
                    keep(2 * q + c, value)
                keep(6 + 2 * q + c, value * degree)
                keep(12 + 2 * q + c, roll_lanes(value * link, -1))
        for c in range(2):
            keep(18 + c, speed_ref[c * GROUP : (c + 1) * GROUP, :] * weight)
        for at in range(20, 24):
            keep(at, jnp.zeros((GROUP, DEG), f32))

    prepare()

    def one(step):
        final = last[pl.ds(step, 1), :]

        slot_small, slot_large, small = pair_orders(map_ref, first, step)
        par = lax.rem(small, 2)
        wide = lax.broadcasted_iota(i32, (24, DEG), 1)

        def load(slot):
            return jnp.concatenate(
                [coefs[t, pl.ds(slot, 24, stride=GROUP), :] for t in range(4)], axis=1
            )

        plain = load(slot_small)
        edge = plain[:, DEG - 1 :]
        north = jnp.where(wide == 0, 0.0, roll_lanes(plain, 1))
        flip = lax.rem(wide + 1 + par, 2) == 0
        south = jnp.where(flip, north, -north)
        north_large = pltpu.roll(load(slot_large), small + 1, 1)
        south_large = jnp.where(lax.rem(wide, 2) == 0, north_large, -north_large)
        high, low = split(jnp.concatenate([north, south, north_large, south_large], axis=0))
        both = jnp.concatenate([high, low], axis=0)
        thirds = []
        for t in range(3):
            product = dot_nn(both[:, : DEG // 2], pair_tile(table, step, 0, t)) + dot_nn(
                both[:, DEG // 2 :], pair_tile(table, step, 1, t)
            )
            thirds.append(product[:96, :128] + (product[96:, :128] + product[:96, 128:]))
        result = jnp.concatenate(thirds, axis=1)
        sign = jnp.where(par == 1, 1.0, -1.0)
        x = lat_ref[0:1, :]
        for which in range(2):
            base = jnp.where(which == 0, par, 1 - par) * 16 + step
            for hemi in range(2):
                at = 48 * which + 24 * hemi
                r = result[at : at + 24]
                if which == 0:
                    r = r + (edge if hemi == 0 else edge * sign) * final
                slant = (x if hemi == 0 else -x) * r[6:12] - r[12:18]
                for q in range(7):
                    for c in range(2):
                        at = 2 * q + c
                        if q < 3:
                            line = r[at : at + 1]
                        elif q < 6:
                            line = slant[at - 6 : at - 5]
                        else:
                            line = r[18 + c : 19 + c]
                        rows[pl.ds(q * 32 + base + 8 * c, 1), hemi * NORTH : (hemi + 1) * NORTH] = line

    def several(step, carry):
        for j in range(UNROLL):
            one(step * UNROLL + j)
        return carry

    lax.fori_loop(0, PAIRS // UNROLL, several, 0)
    for tile in range(6):
        part = []
        for item in range(4 * tile, 4 * tile + 4):
            if item < len(ITEMS):
                q, blk = ITEMS[item]
                part.append(rows[q * 32 : (q + 1) * 32, blk * 256 : (blk + 1) * 256])
            else:
                part.append(jnp.zeros((32, 256), f32))
        turned = jnp.transpose(jnp.concatenate(part, axis=0))
        chunk_ref[:, tile * 8 : tile * 8 + 8, :] = turned.reshape(32, 8, 128)


def near(x):
    return x if INTERPRET else pltpu.with_memory_space_constraint(x, pltpu.VMEM)


def near_out(*shape):
    return jax.ShapeDtypeStruct(shape, f32) if INTERPRET else pltpu.VMEM(shape, f32)


def specs(scalars, arrays):
    return [pl.BlockSpec(memory_space=pltpu.SMEM)] * scalars + [
        pl.BlockSpec(memory_space=pltpu.VMEM)
    ] * arrays


def synthesis(place, orders, psi, temp, mag, speed, lat, norm):
    return pl.pallas_call(
        synthesis_kernel,
        in_specs=specs(2, 6),
        out_shape=jax.ShapeDtypeStruct((32, 48, 128), f32),
        scratch_shapes=[
            pltpu.VMEM((3, DEG * PAIRS, 128), f32),
            pltpu.VMEM((PAIRS, NORTH), f32),
            pltpu.VMEM((4, 24 * GROUP, 128), f32),
            pltpu.VMEM((7 * 32, NLAT), f32),
        ],
        interpret=INTERPRET,
        name="synthesis",
    )(place, orders, psi, temp, mag, speed, lat, norm)


def grid_kernel(place_ref, x_ref, below_ref, above_ref, wave_ref, order_ref, per_ref, out_ref, stage):
    inverse = 1.0 / (2.0 * (SPAN / SHELLS))
    for half in range(2):
        lanes = slice(half * 128, (half + 1) * 128)
        sources = range(half * 16, half * 16 + 16)
        for tile in range(6):
            got = block_swap([x_ref[s, tile * 8 : tile * 8 + 8, :] for s in sources], 8)
            for g in range(16):
                if tile * 4 + g // 4 >= len(ITEMS):
                    continue
                q, blk = ITEMS[tile * 4 + g // 4]
                at = q * 24 + blk * 8
                pc = g % 4
                if q in (1, 2):
                    turn = pc ^ 1
                    m = order_ref[pc // 2 : pc // 2 + 1, lanes]
                    stage[turn, at : at + 8, lanes] = got[g] * (m if pc % 2 == 0 else -m)
                else:
                    stage[pc, at : at + 8, lanes] = got[g]
        for tile in range(2):
            got = block_swap(
                [
                    (above_ref[s, tile * 8 : tile * 8 + 8, :] - below_ref[s, tile * 8 : tile * 8 + 8, :])
                    * inverse
                    for s in sources
                ],
                8,
            )
            for g in range(16):
                item = tile * 4 + g // 4
                if item < 6:
                    q, blk = ITEMS[item]
                    at = (q + 6) * 24 + blk * 8
                    stage[g % 4, at : at + 8, lanes] = got[g]
    tables = [split(wave_ref[pc]) for pc in range(4)]
    waves = []
    for pc in range(4):
        high, low = split(stage[pc])
        wave_high, wave_low = tables[pc]
        waves.append(dot_nn(high, wave_high) + (dot_nn(low, wave_high) + dot_nn(high, wave_low)))
    cos_even, sin_even, cos_odd, sin_odd = waves
    ce, se = cos_even + cos_odd, sin_even + sin_odd
    co, so = cos_even - cos_odd, sin_even - sin_odd
    images = [ce + se, ce - se, co - so, co + so]
    mine = lax.broadcasted_iota(i32, (48, 128), 1) == place_ref[0]
    both = jnp.sum(jnp.where(mine, per_ref[...], 0.0), axis=1, keepdims=True)
    radius = INNER + (SPAN / SHELLS) * (place_ref[1].astype(f32) + 0.5)
    f1 = both[0:24] / jnp.broadcast_to(radius * radius, (24, 1))
    f2 = both[24:48]
    forced = []
    for g in images:
        part = [g[q * 24 : (q + 1) * 24] for q in range(9)]
        heat = (part[3] * part[1] - part[0] * part[4]) * f1 + part[6] * part[7] * f2
        field = (part[3] * part[2] - part[0] * part[5]) * f1 + part[6] * part[8] * f2
        forced.append(jnp.concatenate([heat, field], axis=0))
    a, b = forced[0] + forced[1], forced[2] + forced[3]
    d, e = forced[0] - forced[1], forced[3] - forced[2]
    sides = [a + b, d + e, a - b, d - e]
    for par in range(2):
        parts = []
        for c in range(2):
            pc = par * 2 + c
            high, low = split(sides[pc])
            wave_high, wave_low = tables[pc]
            parts.append(dot_nt(wave_high, high) + (dot_nt(wave_high, low) + dot_nt(wave_low, high)))
        pair = jnp.concatenate(parts + [jnp.zeros((256, 32), f32)], axis=1)
        out_ref[:, par * 8 : par * 8 + 8, :] = pair.reshape(32, 8, 128)


def grid_stage(place, x, below, above, wave, order, per):
    return pl.pallas_call(
        grid_kernel,
        in_specs=specs(1, 6),
        out_shape=jax.ShapeDtypeStruct((32, 16, 128), f32),
        scratch_shapes=[pltpu.VMEM((4, 216, 256), f32)],
        interpret=INTERPRET,
        name="forcing",
    )(place, near(x), near(below), near(above), near(wave), order, per)


def analysis_kernel(
    place_ref, map_ref, v_ref, temp_ref, mag_ref, sub_ref, diag_ref, sup_ref, lat_ref, norm_ref,
    out_ref, table, last, sums, right,
):
    first = place_ref[0] * GROUP
    legendre_table(map_ref, first, lat_ref, norm_ref, table, last)

    def prepare():
        for par in range(2):
            halves = [
                block_swap(
                    [v_ref[half * 16 + s, par * 8 : par * 8 + 8, :] for s in range(16)], 8
                )
                for half in range(2)
            ]
            for c in range(2):
                for f in range(2):
                    tiles = []
                    for blk in range(3):
                        g = c * 6 + f * 3 + blk
                        tiles += [halves[0][g], halves[1][g]]
                    for eo in range(2):
                        at = par * 64 + (eo * 4 + f * 2 + c) * 8
                        for t in range(3):
                            mixed = tiles[t] + tiles[t + 3] if eo == 0 else tiles[t] - tiles[t + 3]
                            sums[t, at : at + 8, :] = mixed

    prepare()

    def one(step):
        slot_small, slot_large, small = pair_orders(map_ref, first, step)
        par = lax.rem(small, 2)

        def load(parity):
            start = parity * 64 + step
            return jnp.concatenate([sums[t, pl.ds(start, 8, stride=8), :] for t in range(3)], axis=1)

        value_small = load(par)
        high, low = split(jnp.concatenate([value_small, load(1 - par)], axis=0))
        zero = jnp.zeros((16, 128), bf16)
        halves = []
        for half in range(2):
            product = 0.0
            for t in range(3):
                cut = slice(t * 128, (t + 1) * 128)
                left = jnp.concatenate(
                    [
                        jnp.concatenate([high[:, cut], high[:, cut]], axis=1),
                        jnp.concatenate([low[:, cut], zero], axis=1),
                    ],
                    axis=0,
                )
                product = product + dot_nt(left, pair_tile(table, step, half, t))
            halves.append(product[:16] + product[16:])
        result = jnp.concatenate(halves, axis=1)
        wide = lax.broadcasted_iota(i32, (4, DEG), 1)
        picked = jnp.where(lax.rem(wide + 1 + par, 2) == 0, result[0:4], result[4:8])
        edge_value = jnp.where(par == 1, value_small[0:4], value_small[4:8])
        edge = jnp.sum(edge_value * last[pl.ds(step, 1), :], axis=1, keepdims=True)
        tendency_small = jnp.where(wide == DEG - 1, edge, roll_lanes(picked, -1))
        tendency_small = jnp.where(wide >= small, tendency_small, 0.0)
        picked = jnp.where(lax.rem(wide, 2) == 0, result[8:12], result[12:16])
        large = DEG - 1 - small
        wide8 = jnp.concatenate([picked, picked], axis=0)
        tendency_large = jnp.where(wide >= large, pltpu.roll(wide8, large, 1)[0:4], 0.0)
        for fc in range(4):
            right[fc, pl.ds(slot_small, 1), :] = tendency_small[fc : fc + 1]
            right[fc, pl.ds(slot_large, 1), :] = tendency_large[fc : fc + 1]

    def several(step, carry):
        for j in range(UNROLL):
            one(step * UNROLL + j)
        return carry

    lax.fori_loop(0, PAIRS // UNROLL, several, 0)
    for fc in range(4):
        f, c = fc // 2, fc % 2
        base = temp_ref if f == 0 else mag_ref
        right[fc, 0:GROUP, :] = base[c * GROUP : (c + 1) * GROUP, :] + STEP * right[fc, 0:GROUP, :]
        right[fc, GROUP : GROUP + 8, :] = jnp.concatenate(
            [ref[f : f + 1, :] for ref in (sub_ref, diag_ref, sup_ref)]
            + [jnp.zeros((5, DEG), f32)],
            axis=0,
        )
    for tile in range(4):
        got = block_swap([right[fc, :, tile * 128 : (tile + 1) * 128] for fc in range(4)], 32)
        for r in range(4):
            out_ref[tile * 4 + r] = got[r]


def analysis(place, orders, v, temp, mag, sub, diag, sup, lat, norm):
    return pl.pallas_call(
        analysis_kernel,
        in_specs=specs(2, 8),
        out_shape=jax.ShapeDtypeStruct((16, 24, 128), f32),
        scratch_shapes=[
            pltpu.VMEM((3, DEG * PAIRS, 128), f32),
            pltpu.VMEM((PAIRS, NORTH), f32),
            pltpu.VMEM((3, 128, 128), f32),
            pltpu.VMEM((4, GROUP + 8, DEG), f32),
        ],
        interpret=INTERPRET,
        name="analysis",
    )(place, orders, near(v), temp, mag, sub, diag, sup, lat, norm)


def solve_kernel(x_ref, out_ref):
    running = jnp.zeros((GROUP, 128), f32)
    scaled = []
    for k in range(SHELLS):
        running = x_ref[k, 0:GROUP, :] + (1.0 - x_ref[k, GROUP : GROUP + 1, :]) * running
        scaled.append(running / x_ref[k, GROUP + 1 : GROUP + 2, :])
    running = jnp.zeros((GROUP, 128), f32)
    for k in reversed(range(SHELLS)):
        running = scaled[k] + (1.0 - x_ref[k, GROUP + 2 : GROUP + 3, :]) * running
        out_ref[k] = running


def solve(x):
    return pl.pallas_call(
        solve_kernel,
        out_shape=near_out(SHELLS, GROUP, 128),
        interpret=INTERPRET,
        compiler_params=pltpu.CompilerParams(vmem_limit_bytes=8 * 2**20),
        name="radial",
    )(near(x))


def gather_kernel(x_ref, temp_ref, mag_ref):
    for tile in range(4):
        got = block_swap([x_ref[tile * 4 + r] for r in range(4)], 32)
        lanes = slice(tile * 128, (tile + 1) * 128)
        for fc in range(4):
            ref = temp_ref if fc < 2 else mag_ref
            c = fc % 2
            ref[c * GROUP : (c + 1) * GROUP, lanes] = got[fc]


def gather_stage(x):
    return pl.pallas_call(
        gather_kernel,
        out_shape=[jax.ShapeDtypeStruct((32, DEG), f32)] * 2,
        interpret=INTERPRET,
        compiler_params=pltpu.CompilerParams(vmem_limit_bytes=8 * 2**20),
        name="assemble",
    )(near(x))


def sorted_orders(orders):
    pair = orders.reshape(DEG // 2, 2)
    even = jnp.where(pair[:, 0] % 2 == 0, pair[:, 0], pair[:, 1])
    return jnp.stack([even, DEG - 1 - even])


def wave_tables(ordered):
    node = 2 * jnp.arange(QUARTER, dtype=i32) + 1
    phase = ordered[:, :, None] * node % (2 * NLON)
    angle = math.pi / NLON * phase.astype(f32)
    return jnp.stack([jnp.cos(angle), -jnp.sin(angle)], axis=1).reshape(4, DEG // 2, QUARTER)


def body(
    toroidal_stream_spectra,
    thermal_spectra,
    induction_potential,
    outward_speed_spectra,
    position_azimuth_map,
    subdiagonal_complement,
    superdiagonal_complement,
    diagonal_entries,
):
    lat, norm, per = map(jnp.asarray, host_tables())
    place = jnp.stack([lax.axis_index("ma"), lax.axis_index("row")]).astype(i32)
    psi, temp, mag, speed = (
        a.reshape(32, DEG)
        for a in (
            toroidal_stream_spectra, thermal_spectra, induction_potential, outward_speed_spectra
        )
    )
    chunk = synthesis(place, position_azimuth_map, psi, temp, mag, speed, lat, norm)
    chunk = lax.all_to_all(chunk, "ma", 0, 0, tiled=True)
    forward = [(i, i + 1) for i in range(SHELLS - 1)]
    profiles = chunk[:, 0:16, :]
    below = lax.ppermute(profiles, "row", forward)
    above = lax.ppermute(profiles, "row", [(b, a) for a, b in forward])
    ordered = sorted_orders(position_azimuth_map)
    spectra = grid_stage(
        place, chunk, below, above, wave_tables(ordered), ordered.astype(f32), per
    )
    spectra = lax.all_to_all(spectra, "ma", 0, 0, tiled=True)
    sub, diag, sup = (
        a.reshape(2, DEG) for a in (subdiagonal_complement, diagonal_entries, superdiagonal_complement)
    )
    right = analysis(
        place, position_azimuth_map, spectra, temp, mag, sub, diag, sup, lat, norm
    )
    right = lax.all_to_all(right, "row", 0, 0, tiled=True)
    solved = lax.all_to_all(solve(right), "row", 0, 0, tiled=True)
    new_temp, new_mag = gather_stage(solved)
    shape = thermal_spectra.shape
    return new_temp.reshape(shape), new_mag.reshape(shape)


def solution(mesh):
    spectra = P(None, "row", "ma", None)
    radial = P(None, "row", None)
    in_specs = (spectra,) * 4 + (P(),) + (radial,) * 3
    return jax.shard_map(
        body, mesh=mesh, in_specs=in_specs, out_specs=(spectra, spectra), check_vma=False
    )
```

time: 144 us -> 115 us (0.80)
  Pallas kernels: 41.5 us -> 18.5 us
  blocking collectives: 36.7 us -> 34.1 us
  local copies, waits for them, and re-layouts: 3.6 us -> 1.6 us
  other arithmetic: 6.45 us -> 4.59 us
  starting transfers between devices: 24.2 us -> 25.9 us
    pallas_call x4, Pallas kernels: 39.8 us -> 17.7 us  [the longest x1 6.89 us: synthesis(): pl.pallas_call(synthesis_kernel, in_specs=specs(2, 6), out_shape=jax.Shap...]
    all_to_all x1, waiting for transfers between devices: 10.2 us -> 8.43 us  [body(): spectra = lax.all_to_all(spectra, 'ma', 0, 0, tiled=True)]
    all_to_all x1, blocking collectives: 24 us -> 22.5 us  [body(): right = lax.all_to_all(right, 'row', 0, 0, tiled=True)]
where the time goes in v1:
time: 115 us
  blocking collectives  34.1 us (30%)
  waiting for transfers between devices  29.2 us (25%)
  starting transfers between devices  25.9 us (23%)
  Pallas kernels  18.5 us (16%)
  other arithmetic  4.59 us (4%)
  local copies, waits for them, and re-layouts  1.6 us (1%)
    all_to_all x1, blocking collectives, body(): right = lax.all_to_all(right, 'row', 0, 0, tiled=True)  22.5 us
    all_to_all x1, waiting for transfers between devices, body(): chunk = lax.all_to_all(chunk, 'ma', 0, 0, tiled=True)  18.4 us
    all_to_all x1, blocking collectives, body(): solved = lax.all_to_all(solve(right), 'row', 0, 0, tiled=True)  11.6 us
    all_to_all x1, starting transfers between devices, body(): chunk = lax.all_to_all(chunk, 'ma', 0, 0, tiled=True)  10.5 us
    ppermute x1, starting transfers between devices, body(): below = lax.ppermute(profiles, 'row', forward)  8.83 us
    all_to_all x1, waiting for transfers between devices, body(): spectra = lax.all_to_all(spectra, 'ma', 0, 0, tiled=True)  8.43 us
    pallas_call x1, Pallas kernels, synthesis(): pl.pallas_call(synthesis_kernel, in_specs=specs(2, 6), out_shape=jax.Shap...  6.89 us
    pallas_call x1, Pallas kernels, analysis(): pl.pallas_call(analysis_kernel, in_specs=specs(2, 8), out_shape=jax.Shape...  6.61 us
  transfers between devices with their start and end apart: 4, of which 3 were waited for; matrix products, arithmetic and copies ran while one was open for 5% of the time, Pallas kernels for 0%

profile of v1, /device:TPU:1, one launch (start us, length us, event | category | flops | bytes accessed | tf_op | source)
XLA Modules:
  0.0 114.6 jit_solution(2016773579066271927)
XLA Ops:
  0.6 0.0 copy-start
  0.6 0.6 pad_add_fusion.1.place_ref
  1.3 6.9 %synthesis.1 = f32[32,48,128]{2,1,0:T(8,128)} custom-call(s32[2]{0:T(128)} %pad_add_fusion.1.place_ref, s32[512]{0:T(512)} %map_ref.3, f32[32,512]{1,0:T(8,128)} %bitcast.27, f32[32,512]{1,0:T(8,128)} %bitcast.23, f32[32,512]{1,0:T(8,128)} %bitcast.25, f32[32,512]{1,0:T(8,128)} %bitcast.28, f32[8,384]{1,0:T(8,128)} %constant.48.clone.lat_ref, ...), custom_call_target="tpu_custom_call" | custom-call | tf_op jit(solution)/shard_map/synthesis/pallas_call | solution.py:298
  8.2 10.5 %all-to-all-start = ((f32[32,48,128]{2,1,0:T(8,128)}), f32[32,48,128]{2,1,0:T(8,128)S(1)}, u32[]{:S(2)}, u32[]{:S(2)}) async-start(f32[32,48,128]{2,1,0:T(8,128)} %synthesis.1), calls=%async_computation | async-start | bytes 1572864 | tf_op jit(solution)/shard_map/all_to_all | solution.py:573
  18.6 0.0 copy-done
  18.7 0.1 reshape.174
  18.8 0.2 slice_reduce_fusion
  19.1 0.6 fusion.7
  19.6 18.4 %all-to-all-done.x_ref = f32[32,48,128]{2,1,0:T(8,128)S(1)} async-done(((f32[32,48,128]{2,1,0:T(8,128)}), f32[32,48,128]{2,1,0:T(8,128)S(1)}, u32[]{:S(2)}, u32[]{:S(2)}) %all-to-all-start) | async-done | bytes 786464 | tf_op jit(solution)/shard_map/all_to_all | solution.py:573
  38.0 8.8 %collective-permute-start = (f32[32,16,128]{2,1,0:T(8,128)S(1)}, f32[32,16,128]{2,1,0:T(8,128)S(1)}, u32[]{:S(2)}, u32[]{:S(2)}) collective-permute-start(f32[32,16,128]{2,1,0:T(8,128)S(1)} %slice.13), channel_id=1, source_target_pairs={{0,32},{32,64},{64,96},{96,128},{128,160},{160,192},{192,224},{224... | collective-permute-start | bytes 786440 | tf_op jit(solution)/shard_map/ppermute | solution.py:576
  46.9 1.9 %collective-permute-start.1 = (f32[32,16,128]{2,1,0:T(8,128)S(1)}, f32[32,16,128]{2,1,0:T(8,128)S(1)}, u32[]{:S(2)}, u32[]{:S(2)}) collective-permute-start(f32[32,16,128]{2,1,0:T(8,128)S(1)} %slice.13), channel_id=1, source_target_pairs={{32,0},{64,32},{96,64},{128,96},{160,128},{192,160},{224,192},{256... | collective-permute-start | bytes 786440 | tf_op jit(solution)/shard_map/ppermute | solution.py:577
  48.8 3.3 %fusion.4 = (f32[2,1,256,384]{3,2,1,0:T(8,128)S(1)}, f32[2,1,256,384]{3,2,1,0:T(8,128)S(1)}) fusion(s32[384]{0:T(512)S(1)} %multiply_add_fusion, s32[2,256]{1,0:T(2,128)S(1)} %get-tuple-element.17), kind=kLoop, calls=%fused_computation.8 | loop fusion | flops 1966080 | bytes 1576448 | tf_op jit(solution)/shard_map/cos | solution.py:551
  52.1 0.1 pad_maximum_fusion
  52.2 0.0 collective-permute-done.below_ref
  52.2 2.4 %collective-permute-done.1.above_ref = f32[32,16,128]{2,1,0:T(8,128)S(1)} collective-permute-done((f32[32,16,128]{2,1,0:T(8,128)S(1)}, f32[32,16,128]{2,1,0:T(8,128)S(1)}, u32[]{:S(2)}, u32[]{:S(2)}) %collective-permute-start.1) | collective-permute-done | bytes 262176 | tf_op jit(solution)/shard_map/ppermute | solution.py:577
  54.6 0.0 copy-start.1
  54.6 0.0 copy-start.2
  54.6 0.0 copy-start.3
  54.6 4.1 %forcing.1 = f32[32,16,128]{2,1,0:T(8,128)} custom-call(s32[2]{0:T(128)} %pad_add_fusion.1.place_ref, f32[32,48,128]{2,1,0:T(8,128)S(1)} %all-to-all-done.x_ref, f32[32,16,128]{2,1,0:T(8,128)S(1)} %collective-permute-done.below_ref, f32[32,16,128]{2,1,0:T(8,128)S(1)} %collective-permute-done.1.above_ref, f32[4,256,384]{2,1,0:T(8,128)S(1)} %bitcast.22, ...), custom_call_target="tpu_custom_call" | custom-call | tf_op jit(solution)/shard_map/forcing/pallas_call | solution.py:383
  58.7 4.6 %all-to-all-start.1 = ((f32[32,16,128]{2,1,0:T(8,128)}), f32[32,16,128]{2,1,0:T(8,128)S(1)}, u32[]{:S(2)}, u32[]{:S(2)}) async-start(f32[32,16,128]{2,1,0:T(8,128)} %forcing.1), calls=%async_computation.1 | async-start | bytes 524288 | tf_op jit(solution)/shard_map/all_to_all | solution.py:582
  63.3 0.0 copy-done.1
  63.3 0.6 copy.23
  63.9 0.0 copy-done.2
  63.9 0.0 copy-done.3
  64.0 0.6 copy_bitcast_fusion
  64.6 8.4 %all-to-all-done.1.v_ref = f32[32,16,128]{2,1,0:T(8,128)S(1)} async-done(((f32[32,16,128]{2,1,0:T(8,128)}), f32[32,16,128]{2,1,0:T(8,128)S(1)}, u32[]{:S(2)}, u32[]{:S(2)}) %all-to-all-start.1) | async-done | bytes 262176 | tf_op jit(solution)/shard_map/all_to_all | solution.py:582
  73.0 6.6 %analysis.1 = f32[16,24,128]{2,1,0:T(8,128)} custom-call(s32[2]{0:T(128)} %pad_add_fusion.1.place_ref, s32[512]{0:T(512)} %map_ref.3, f32[32,16,128]{2,1,0:T(8,128)S(1)} %all-to-all-done.1.v_ref, f32[32,512]{1,0:T(8,128)} %bitcast.24, f32[32,512]{1,0:T(8,128)} %bitcast.26, f32[2,512]{1,0:T(2,128)} %bitcast.29, f32[2,512]{1,0:T(2,128)} %get-tuple-element.19.diag_ref, ...), custom_call_target="tpu_custom_call" | custom-call | tf_op jit(solution)/shard_map/analysis/pallas_call | solution.py:484
  79.6 22.5 %all_to_all.20.x_ref = f32[16,24,128]{2,1,0:T(8,128)S(1)} all-to-all(f32[16,24,128]{2,1,0:T(8,128)} %analysis.1), channel_id=1, replica_groups=mesh['row'=16,'ma'=32] {'row'}, dimensions={0} | all-to-all | bytes 393216 | tf_op jit(solution)/shard_map/all_to_all | solution.py:589
  102.0 0.1 radial.1
  102.1 11.6 %all_to_all.21.x_ref = f32[16,16,128]{2,1,0:T(8,128)S(1)} all-to-all(f32[16,16,128]{2,1,0:T(8,128)S(1)} %radial.1), channel_id=1, replica_groups=mesh['row'=16,'ma'=32] {'row'}, dimensions={0} | all-to-all | bytes 262144 | tf_op jit(solution)/shard_map/all_to_all | solution.py:590
  113.8 0.8 assemble.1
  (3 shorter events, 0.0 us)
Async XLA Ops:
  0.6 18.0 %copy-start = (s32[512]{0:T(512)S(1)}, s32[512]{0:T(512)}, u32[]{:S(2)}) copy-start(s32[512]{0:T(512)} %map_ref.3) | copy-start | bytes 6148
  8.2 29.9 %all-to-all-start = ((f32[32,48,128]{2,1,0:T(8,128)}), f32[32,48,128]{2,1,0:T(8,128)S(1)}, u32[]{:S(2)}, u32[]{:S(2)}) async-start(f32[32,48,128]{2,1,0:T(8,128)} %synthesis.1), calls=%async_computation | async-start | bytes 1572864 | tf_op jit(solution)/shard_map/all_to_all | solution.py:573
  38.0 14.1 %collective-permute-start = (f32[32,16,128]{2,1,0:T(8,128)S(1)}, f32[32,16,128]{2,1,0:T(8,128)S(1)}, u32[]{:S(2)}, u32[]{:S(2)}) collective-permute-start(f32[32,16,128]{2,1,0:T(8,128)S(1)} %slice.13), channel_id=1, source_target_pairs={{0,32},{32,64},{64,96},{96,128},{128,160},{160,192},{192,224},{224... | collective-permute-start | bytes 786440 | tf_op jit(solution)/shard_map/ppermute | solution.py:576
  46.9 7.7 %collective-permute-start.1 = (f32[32,16,128]{2,1,0:T(8,128)S(1)}, f32[32,16,128]{2,1,0:T(8,128)S(1)}, u32[]{:S(2)}, u32[]{:S(2)}) collective-permute-start(f32[32,16,128]{2,1,0:T(8,128)S(1)} %slice.13), channel_id=1, source_target_pairs={{32,0},{64,32},{96,64},{128,96},{160,128},{192,160},{224,192},{256... | collective-permute-start | bytes 786440 | tf_op jit(solution)/shard_map/ppermute | solution.py:577
  54.6 8.8 %copy-start.1 = (f32[2,1,512]{2,1,0:T(1,128)S(1)}, f32[2,1,512]{2,1,0:T(1,128)}, u32[]{:S(2)}) copy-start(f32[2,1,512]{2,1,0:T(1,128)} %param.16) | copy-start | bytes 12292
  54.6 9.4 %copy-start.2 = (f32[2,1,512]{2,1,0:T(1,128)S(1)}, f32[2,1,512]{2,1,0:T(1,128)}, u32[]{:S(2)}) copy-start(f32[2,1,512]{2,1,0:T(1,128)} %param.17) | copy-start | bytes 12292
  54.6 9.4 %copy-start.3 = (f32[2,1,512]{2,1,0:T(1,128)S(1)}, f32[2,1,512]{2,1,0:T(1,128)}, u32[]{:S(2)}) copy-start(f32[2,1,512]{2,1,0:T(1,128)} %param.18) | copy-start | bytes 12292
  58.7 14.3 %all-to-all-start.1 = ((f32[32,16,128]{2,1,0:T(8,128)}), f32[32,16,128]{2,1,0:T(8,128)S(1)}, u32[]{:S(2)}, u32[]{:S(2)}) async-start(f32[32,16,128]{2,1,0:T(8,128)} %forcing.1), calls=%async_computation.1 | async-start | bytes 524288 | tf_op jit(solution)/shard_map/all_to_all | solution.py:582

commit v2 on v1

--- a/solution.py
+++ b/solution.py
@@ -298,7 +298,7 @@
     return pl.pallas_call(
         synthesis_kernel,
         in_specs=specs(2, 6),
-        out_shape=jax.ShapeDtypeStruct((32, 48, 128), f32),
+        out_shape=near_out(32, 48, 128),
         scratch_shapes=[
             pltpu.VMEM((3, DEG * PAIRS, 128), f32),
             pltpu.VMEM((PAIRS, NORTH), f32),
@@ -310,13 +310,25 @@
     )(place, orders, psi, temp, mag, speed, lat, norm)
 
 
-def grid_kernel(place_ref, x_ref, below_ref, above_ref, wave_ref, order_ref, per_ref, out_ref, stage):
-    inverse = 1.0 / (2.0 * (SPAN / SHELLS))
+def spread(tables, stage, rows):
+    waves = []
+    for pc in range(4):
+        high, low = split(stage[pc, 0:rows, :])
+        wave_high, wave_low = tables[pc]
+        waves.append(dot_nn(high, wave_high) + (dot_nn(low, wave_high) + dot_nn(high, wave_low)))
+    cos_even, sin_even, cos_odd, sin_odd = waves
+    ce, se = cos_even + cos_odd, sin_even + sin_odd
+    co, so = cos_even - cos_odd, sin_even - sin_odd
+    return [ce + se, ce - se, co - so, co + so]
+
+
+def flow_kernel(place_ref, shell_ref, x_ref, wave_ref, order_ref, per_ref, out_ref, stage):
     for half in range(2):
         lanes = slice(half * 128, (half + 1) * 128)
-        sources = range(half * 16, half * 16 + 16)
         for tile in range(6):
-            got = block_swap([x_ref[s, tile * 8 : tile * 8 + 8, :] for s in sources], 8)
+            got = block_swap(
+                [x_ref[s, tile * 8 : tile * 8 + 8, :] for s in range(half * 16, half * 16 + 16)], 8
+            )
             for g in range(16):
                 if tile * 4 + g // 4 >= len(ITEMS):
                     continue
@@ -329,12 +341,43 @@
                     stage[turn, at : at + 8, lanes] = got[g] * (m if pc % 2 == 0 else -m)
                 else:
                     stage[pc, at : at + 8, lanes] = got[g]
+    tables = [split(wave_ref[pc]) for pc in range(4)]
+    images = spread(tables, stage, 7 * 24)
+    mine = lax.broadcasted_iota(i32, (48, 128), 1) == place_ref[0]
+    both = jnp.sum(jnp.where(mine, per_ref[...], 0.0), axis=1, keepdims=True)
+    radius = INNER + (SPAN / SHELLS) * (shell_ref[0].astype(f32) + 0.5)
+    f1 = both[0:24] / jnp.broadcast_to(radius * radius, (24, 1))
+    f2 = both[24:48]
+    for n, g in enumerate(images):
+        part = [g[q * 24 : (q + 1) * 24] for q in range(7)]
+        out_ref[n, 0:24, :] = (part[3] * part[1] - part[0] * part[4]) * f1
+        out_ref[n, 24:48, :] = (part[3] * part[2] - part[0] * part[5]) * f1
+        out_ref[n, 48:72, :] = part[6] * f2
+
+
+def flow_stage(place, shell, x, wave, order, per):
+    return pl.pallas_call(
+        flow_kernel,
+        in_specs=specs(2, 4),
+        out_shape=near_out(4, 72, QUARTER),
+        scratch_shapes=[pltpu.VMEM((4, 7 * 24, 256), f32)],
+        interpret=INTERPRET,
+        compiler_params=pltpu.CompilerParams(vmem_limit_bytes=24 * 2**20),
+        name="flow",
+    )(place, shell, near(x), near(wave), order, per)
+
+
+def forcing_kernel(shell_ref, chip_ref, link_ref, wave_ref, flow_ref, out_ref, stage):
+    even = lax.rem(shell_ref[0], 2) == 0
+    inverse = jnp.where(even, 1.0, -1.0) / (2.0 * (SPAN / SHELLS))
+    for half in range(2):
+        lanes = slice(half * 128, (half + 1) * 128)
         for tile in range(2):
+            rows = slice(tile * 8, tile * 8 + 8)
             got = block_swap(
                 [
-                    (above_ref[s, tile * 8 : tile * 8 + 8, :] - below_ref[s, tile * 8 : tile * 8 + 8, :])
-                    * inverse
-                    for s in sources
+                    (chip_ref[s, rows, :] - link_ref[s, rows, :]) * inverse
+                    for s in range(half * 16, half * 16 + 16)
                 ],
                 8,
             )
@@ -342,28 +385,14 @@
                 item = tile * 4 + g // 4
                 if item < 6:
                     q, blk = ITEMS[item]
-                    at = (q + 6) * 24 + blk * 8
+                    at = (q - 1) * 24 + blk * 8
                     stage[g % 4, at : at + 8, lanes] = got[g]
     tables = [split(wave_ref[pc]) for pc in range(4)]
-    waves = []
-    for pc in range(4):
-        high, low = split(stage[pc])
-        wave_high, wave_low = tables[pc]
-        waves.append(dot_nn(high, wave_high) + (dot_nn(low, wave_high) + dot_nn(high, wave_low)))
-    cos_even, sin_even, cos_odd, sin_odd = waves
-    ce, se = cos_even + cos_odd, sin_even + sin_odd
-    co, so = cos_even - cos_odd, sin_even - sin_odd
-    images = [ce + se, ce - se, co - so, co + so]
-    mine = lax.broadcasted_iota(i32, (48, 128), 1) == place_ref[0]
-    both = jnp.sum(jnp.where(mine, per_ref[...], 0.0), axis=1, keepdims=True)
-    radius = INNER + (SPAN / SHELLS) * (place_ref[1].astype(f32) + 0.5)
-    f1 = both[0:24] / jnp.broadcast_to(radius * radius, (24, 1))
-    f2 = both[24:48]
     forced = []
-    for g in images:
-        part = [g[q * 24 : (q + 1) * 24] for q in range(9)]
-        heat = (part[3] * part[1] - part[0] * part[4]) * f1 + part[6] * part[7] * f2
-        field = (part[3] * part[2] - part[0] * part[5]) * f1 + part[6] * part[8] * f2
+    for n, g in enumerate(spread(tables, stage, 48)):
+        speed = flow_ref[n, 48:72, :]
+        heat = flow_ref[n, 0:24, :] + speed * g[0:24]
+        field = flow_ref[n, 24:48, :] + speed * g[24:48]
         forced.append(jnp.concatenate([heat, field], axis=0))
     a, b = forced[0] + forced[1], forced[2] + forced[3]
     d, e = forced[0] - forced[1], forced[3] - forced[2]
@@ -379,23 +408,66 @@
         out_ref[:, par * 8 : par * 8 + 8, :] = pair.reshape(32, 8, 128)
 
 
-def grid_stage(place, x, below, above, wave, order, per):
+def forcing_stage(shell, chip, link, wave, flow):
     return pl.pallas_call(
-        grid_kernel,
-        in_specs=specs(1, 6),
-        out_shape=jax.ShapeDtypeStruct((32, 16, 128), f32),
-        scratch_shapes=[pltpu.VMEM((4, 216, 256), f32)],
+        forcing_kernel,
+        in_specs=specs(1, 4),
+        out_shape=near_out(32, 16, 128),
+        scratch_shapes=[pltpu.VMEM((4, 48, 256), f32)],
         interpret=INTERPRET,
+        compiler_params=pltpu.CompilerParams(vmem_limit_bytes=24 * 2**20),
         name="forcing",
-    )(place, near(x), near(below), near(above), near(wave), order, per)
+    )(shell, near(chip), near(link), near(wave), near(flow))
+
+
+def table_kernel(place_ref, map_ref, lat_ref, norm_ref, after_ref, tab_ref, last, table, ready, sems):
+    legendre_table(map_ref, place_ref[0] * GROUP, lat_ref, norm_ref, table, last)
+    copies = []
+    for pair in range(PAIRS):
+        for half in range(2):
+            rows = slice(half * (DEG // 2), (half + 1) * (DEG // 2))
+            for t in range(3):
+                start = half * (DEG // 2) * PAIRS + pair
+                turned = jnp.transpose(table[t, pl.ds(start, DEG // 2, stride=PAIRS), :])
+                high, low = split(turned)
+                ready[pair, t * 256 : t * 256 + 128, rows] = high
+                ready[pair, t * 256 + 128 : (t + 1) * 256, rows] = low
+        copy = pltpu.make_async_copy(ready.at[pair], tab_ref.at[pair], sems.at[pair])
+        copy.start()
+        copies.append(copy)
+    for copy in copies:
+        copy.wait()
+
+
+def tables(place, orders, lat, norm, after):
+    return pl.pallas_call(
+        table_kernel,
+        in_specs=specs(2, 2) + [pl.BlockSpec(memory_space=pl.ANY)],
+        out_specs=[pl.BlockSpec(memory_space=pl.ANY), pl.BlockSpec(memory_space=pltpu.VMEM)],
+        out_shape=[
+            jax.ShapeDtypeStruct((PAIRS, 2 * NORTH, DEG), bf16),
+            jax.ShapeDtypeStruct((PAIRS, NORTH), f32),
+        ],
+        scratch_shapes=[
+            pltpu.VMEM((3, DEG * PAIRS, 128), f32),
+            pltpu.VMEM((PAIRS, 2 * NORTH, DEG), bf16),
+            pltpu.SemaphoreType.DMA((PAIRS,)),
+        ],
+        interpret=INTERPRET,
+        name="legendre",
+    )(place, orders, lat, norm, after)
 
 
 def analysis_kernel(
-    place_ref, map_ref, v_ref, temp_ref, mag_ref, sub_ref, diag_ref, sup_ref, lat_ref, norm_ref,
-    out_ref, table, last, sums, right,
+    place_ref, map_ref, v_ref, temp_ref, mag_ref, sub_ref, diag_ref, sup_ref, last, tab_ref,
+    out_ref, ready, sums, right, sems,
 ):
     first = place_ref[0] * GROUP
-    legendre_table(map_ref, first, lat_ref, norm_ref, table, last)
+    copies = [
+        pltpu.make_async_copy(tab_ref.at[pair], ready.at[pair], sems.at[pair]) for pair in range(PAIRS)
+    ]
+    for copy in copies:
+        copy.start()
 
     def prepare():
         for par in range(2):
@@ -442,7 +514,8 @@
                     ],
                     axis=0,
                 )
-                product = product + dot_nt(left, pair_tile(table, step, half, t))
+                rows = slice(half * (DEG // 2), (half + 1) * (DEG // 2))
+                product = product + dot_nn(left, ready[step, t * 256 : (t + 1) * 256, rows])
             halves.append(product[:16] + product[16:])
         result = jnp.concatenate(halves, axis=1)
         wide = lax.broadcasted_iota(i32, (4, DEG), 1)
@@ -459,12 +532,9 @@
             right[fc, pl.ds(slot_small, 1), :] = tendency_small[fc : fc + 1]
             right[fc, pl.ds(slot_large, 1), :] = tendency_large[fc : fc + 1]
 
-    def several(step, carry):
-        for j in range(UNROLL):
-            one(step * UNROLL + j)
-        return carry
-
-    lax.fori_loop(0, PAIRS // UNROLL, several, 0)
+    for pair in range(PAIRS):
+        copies[pair].wait()
+        one(pair)
     for fc in range(4):
         f, c = fc // 2, fc % 2
         base = temp_ref if f == 0 else mag_ref
@@ -480,20 +550,20 @@
             out_ref[tile * 4 + r] = got[r]
 
 
-def analysis(place, orders, v, temp, mag, sub, diag, sup, lat, norm):
+def analysis(place, orders, v, temp, mag, sub, diag, sup, last, tab):
     return pl.pallas_call(
         analysis_kernel,
-        in_specs=specs(2, 8),
-        out_shape=jax.ShapeDtypeStruct((16, 24, 128), f32),
+        in_specs=specs(2, 7) + [pl.BlockSpec(memory_space=pl.ANY)],
+        out_shape=near_out(16, 24, 128),
         scratch_shapes=[
-            pltpu.VMEM((3, DEG * PAIRS, 128), f32),
-            pltpu.VMEM((PAIRS, NORTH), f32),
+            pltpu.VMEM((PAIRS, 2 * NORTH, DEG), bf16),
             pltpu.VMEM((3, 128, 128), f32),
             pltpu.VMEM((4, GROUP + 8, DEG), f32),
+            pltpu.SemaphoreType.DMA((PAIRS,)),
         ],
         interpret=INTERPRET,
         name="analysis",
-    )(place, orders, near(v), temp, mag, sub, diag, sup, lat, norm)
+    )(place, orders, near(v), temp, mag, sub, diag, sup, last, tab)
 
 
 def solve_kernel(x_ref, out_ref):
@@ -562,7 +632,8 @@
     diagonal_entries,
 ):
     lat, norm, per = map(jnp.asarray, host_tables())
-    place = jnp.stack([lax.axis_index("ma"), lax.axis_index("row")]).astype(i32)
+    place = lax.axis_index("ma").reshape(1).astype(i32)
+    shell = lax.axis_index("row").reshape(1).astype(i32)
     psi, temp, mag, speed = (
         a.reshape(32, DEG)
         for a in (
@@ -570,21 +641,25 @@
         )
     )
     chunk = synthesis(place, position_azimuth_map, psi, temp, mag, speed, lat, norm)
+    tab, last = tables(place, position_azimuth_map, lat, norm, chunk)
     chunk = lax.all_to_all(chunk, "ma", 0, 0, tiled=True)
-    forward = [(i, i + 1) for i in range(SHELLS - 1)]
+    ordered = sorted_orders(position_azimuth_map)
+    wave = wave_tables(ordered)
+    chunk, wave, tab, last = lax.optimization_barrier((chunk, wave, tab, last))
     profiles = chunk[:, 0:16, :]
-    below = lax.ppermute(profiles, "row", forward)
-    above = lax.ppermute(profiles, "row", [(b, a) for a, b in forward])
-    ordered = sorted_orders(position_azimuth_map)
-    spectra = grid_stage(
-        place, chunk, below, above, wave_tables(ordered), ordered.astype(f32), per
-    )
+    near_pairs = [(i, i ^ 1) for i in range(SHELLS)]
+    far_pairs = [(i, i + 1) for i in range(1, SHELLS - 1, 2)]
+    far_pairs += [(b, a) for a, b in far_pairs]
+    link = lax.ppermute(profiles, "row", far_pairs)
+    chip = lax.ppermute(profiles, "row", near_pairs)
+    flow = flow_stage(place, shell, chunk, wave, ordered.astype(f32), per)
+    spectra = forcing_stage(shell, chip, link, wave, flow)
     spectra = lax.all_to_all(spectra, "ma", 0, 0, tiled=True)
     sub, diag, sup = (
         a.reshape(2, DEG) for a in (subdiagonal_complement, diagonal_entries, superdiagonal_complement)
     )
     right = analysis(
-        place, position_azimuth_map, spectra, temp, mag, sub, diag, sup, lat, norm
+        place, position_azimuth_map, spectra, temp, mag, sub, diag, sup, last, tab
     )
     right = lax.all_to_all(right, "row", 0, 0, tiled=True)
     solved = lax.all_to_all(solve(right), "row", 0, 0, tiled=True)

time: 115 us -> 111 us (0.965)
  waiting for transfers between devices: 29.2 us -> 19.7 us
  Pallas kernels: 18.5 us -> 23.5 us
  blocking collectives: 34.1 us -> 35.6 us
  other arithmetic: 4.59 us -> 3.39 us
    all_to_all x1, waiting for transfers between devices: 18.4 us -> 8.74 us  [body(): chunk = lax.all_to_all(chunk, 'ma', 0, 0, tiled=True)]
    pallas_call x3 -> x5, Pallas kernels: 17.6 us -> 22.7 us  [the longest x1 6.92 us: synthesis(): pl.pallas_call(synthesis_kernel, in_specs=specs(2, 6), out_shape=near_out...]
    all_to_all x1, blocking collectives: 22.5 us -> 23.9 us  [body(): right = lax.all_to_all(right, 'row', 0, 0, tiled=True)]
  transfers between devices with their start and end apart: 4 -> 4, of which waited for: 3 -> 3; matrix products, arithmetic and copies ran while one was open for 5% -> 4% of each run, Pallas kernels for 0% -> 7%
where the time goes in v2:
time: 111 us
  blocking collectives  35.6 us (32%)
  starting transfers between devices  25.9 us (23%)
  Pallas kernels  23.5 us (21%)
  waiting for transfers between devices  19.7 us (18%)
  other arithmetic  3.39 us (3%)
  local copies, waits for them, and re-layouts  1.61 us (1%)
    all_to_all x1, blocking collectives, body(): right = lax.all_to_all(right, 'row', 0, 0, tiled=True)  23.9 us
    all_to_all x1, blocking collectives, body(): solved = lax.all_to_all(solve(right), 'row', 0, 0, tiled=True)  11.6 us
    all_to_all x1, starting transfers between devices, body(): chunk = lax.all_to_all(chunk, 'ma', 0, 0, tiled=True)  10.7 us
    all_to_all x1, waiting for transfers between devices, body(): chunk = lax.all_to_all(chunk, 'ma', 0, 0, tiled=True)  8.74 us
    all_to_all x1, waiting for transfers between devices, body(): spectra = lax.all_to_all(spectra, 'ma', 0, 0, tiled=True)  8.52 us
    pallas_call x1, Pallas kernels, synthesis(): pl.pallas_call(synthesis_kernel, in_specs=specs(2, 6), out_shape=near_out...  6.92 us
    ppermute x1, starting transfers between devices, body(): chip = lax.ppermute(profiles, 'row', near_pairs)  6.85 us
    pallas_call x1, Pallas kernels, tables(): pl.pallas_call(table_kernel, in_specs=specs(2, 2) + [pl.BlockSpec(memory_...  6.62 us
  transfers between devices with their start and end apart: 4, of which 3 were waited for; matrix products, arithmetic and copies ran while one was open for 4% of the time, Pallas kernels for 7%

profile of v2, /device:TPU:1, one launch (start us, length us, event | category | flops | bytes accessed | tf_op | source)
XLA Modules:
  0.0 110.5 jit_solution(13239124870285371490)
XLA Ops:
  0.6 0.0 copy-start.1
  0.6 6.9 %synthesis.1.after_ref = f32[32,48,128]{2,1,0:T(8,128)} custom-call(s32[1]{0:T(128)} %bitcast.place_ref, s32[512]{0:T(512)} %map_ref.5, f32[32,512]{1,0:T(8,128)} %bitcast.28, f32[32,512]{1,0:T(8,128)} %bitcast.24, f32[32,512]{1,0:T(8,128)} %bitcast.26, f32[32,512]{1,0:T(8,128)} %bitcast.29, f32[8,384]{1,0:T(8,128)} %constant.48.clone.lat_ref, ...), custom_call_target="tpu_custom_call" | custom-call | tf_op jit(solution)/shard_map/synthesis/pallas_call | solution.py:298
  7.6 10.7 %all-to-all-start = ((f32[32,48,128]{2,1,0:T(8,128)}), f32[32,48,128]{2,1,0:T(8,128)S(1)}, u32[]{:S(2)}, u32[]{:S(2)}) async-start(f32[32,48,128]{2,1,0:T(8,128)} %synthesis.1.after_ref), calls=%async_computation | async-start | bytes 1572864 | tf_op jit(solution)/shard_map/all_to_all | solution.py:645
  18.2 0.0 copy-done.1
  18.3 0.1 reshape.182
  18.4 6.6 %legendre.1 = (bf16[8,768,512]{2,1,0:T(8,128)(2,1)}, f32[8,384]{1,0:T(8,128)}) custom-call(s32[1]{0:T(128)} %bitcast.place_ref, s32[512]{0:T(512)} %map_ref.5, f32[8,384]{1,0:T(8,128)} %constant.48.clone.lat_ref, f32[8,512]{1,0:T(8,128)} %constant.49.clone.norm_ref, f32[32,48,128]{2,1,0:T(8,128)} %synthesis.1.after_ref), custom_call_target="tpu_custom_call" | custom-call | tf_op jit(solution)/shard_map/legendre/pallas_call | solution.py:443
  25.0 0.2 slice_reduce_fusion
  25.3 3.3 %fusion.4 = (f32[2,1,256,384]{3,2,1,0:T(8,128)S(1)}, f32[2,1,256,384]{3,2,1,0:T(8,128)S(1)}) fusion(s32[384]{0:T(512)S(1)} %multiply_add_fusion, s32[2,256]{1,0:T(2,128)S(1)} %get-tuple-element.29), kind=kLoop, calls=%fused_computation.8 | loop fusion | flops 1966080 | bytes 1576448 | tf_op jit(solution)/shard_map/cos | solution.py:621
  28.6 0.0 copy-start
  28.6 0.1 pad_maximum_fusion
  28.7 8.7 %all-to-all-done.x_ref = f32[32,48,128]{2,1,0:T(8,128)S(1)} async-done(((f32[32,48,128]{2,1,0:T(8,128)}), f32[32,48,128]{2,1,0:T(8,128)S(1)}, u32[]{:S(2)}, u32[]{:S(2)}) %all-to-all-start) | async-done | bytes 786464 | tf_op jit(solution)/shard_map/all_to_all | solution.py:645
  37.5 6.8 %collective-permute-start = (f32[32,16,128]{2,1,0:T(8,128)S(1)}, f32[32,16,128]{2,1,0:T(8,128)S(1)}, u32[]{:S(2)}, u32[]{:S(2)}) collective-permute-start(f32[32,16,128]{2,1,0:T(8,128)S(1)} %slice.12), channel_id=1, source_target_pairs={{0,32},{32,0},{64,96},{96,64},{128,160},{160,128},{192,224},{224,1... | collective-permute-start | bytes 786440 | tf_op jit(solution)/shard_map/ppermute | solution.py:654
  44.3 3.9 %collective-permute-start.1 = (f32[32,16,128]{2,1,0:T(8,128)S(1)}, f32[32,16,128]{2,1,0:T(8,128)S(1)}, u32[]{:S(2)}, u32[]{:S(2)}) collective-permute-start(f32[32,16,128]{2,1,0:T(8,128)S(1)} %slice.12), channel_id=1, source_target_pairs={{32,64},{96,128},{160,192},{224,256},{288,320},{352,384},{416,448}... | collective-permute-start | bytes 786440 | tf_op jit(solution)/shard_map/ppermute | solution.py:653
  48.2 0.0 copy-done
  48.2 1.5 %flow.1.flow_ref = f32[4,72,384]{2,1,0:T(8,128)S(1)} custom-call(s32[1]{0:T(128)} %bitcast.place_ref, s32[1]{0:T(128)} %bitcast.1.shell_ref, f32[32,48,128]{2,1,0:T(8,128)S(1)} %all-to-all-done.x_ref, f32[4,256,384]{2,1,0:T(8,128)S(1)} %bitcast.22, f32[2,256]{1,0:T(2,128)S(1)} %get-tuple-element.28.order_ref, f32[48,128]{1,0:T(8,128)S(1)} %copy-done), custom_call_target="tpu_custom_call" | custom-call | tf_op jit(solution)/shard_map/flow/pallas_call | solution.py:359
  49.8 0.0 copy-start.2
  49.8 0.0 copy-start.3
  49.8 0.0 copy-start.4
  49.8 0.0 collective-permute-done.chip_ref
  49.8 2.4 %collective-permute-done.1.link_ref = f32[32,16,128]{2,1,0:T(8,128)S(1)} collective-permute-done((f32[32,16,128]{2,1,0:T(8,128)S(1)}, f32[32,16,128]{2,1,0:T(8,128)S(1)}, u32[]{:S(2)}, u32[]{:S(2)}) %collective-permute-start.1) | collective-permute-done | bytes 262176 | tf_op jit(solution)/shard_map/ppermute | solution.py:653
  52.3 2.5 %forcing.1 = f32[32,16,128]{2,1,0:T(8,128)} custom-call(s32[1]{0:T(128)} %bitcast.1.shell_ref, f32[32,16,128]{2,1,0:T(8,128)S(1)} %collective-permute-done.chip_ref, f32[32,16,128]{2,1,0:T(8,128)S(1)} %collective-permute-done.1.link_ref, f32[4,256,384]{2,1,0:T(8,128)S(1)} %bitcast.23, f32[4,72,384]{2,1,0:T(8,128)S(1)} %flow.1.flow_ref), custom_call_target="tpu_custom_call" | custom-call | tf_op jit(solution)/shard_map/forcing/pallas_call | solution.py:412
  54.7 4.5 %all-to-all-start.1 = ((f32[32,16,128]{2,1,0:T(8,128)}), f32[32,16,128]{2,1,0:T(8,128)S(1)}, u32[]{:S(2)}, u32[]{:S(2)}) async-start(f32[32,16,128]{2,1,0:T(8,128)} %forcing.1), calls=%async_computation.1 | async-start | bytes 524288 | tf_op jit(solution)/shard_map/all_to_all | solution.py:657
  59.2 0.0 copy-done.2
  59.2 0.6 copy.23
  59.8 0.0 copy-done.3
  59.8 0.0 copy-done.4
  59.8 0.6 copy_bitcast_fusion
  60.4 8.5 %all-to-all-done.1.v_ref = f32[32,16,128]{2,1,0:T(8,128)S(1)} async-done(((f32[32,16,128]{2,1,0:T(8,128)}), f32[32,16,128]{2,1,0:T(8,128)S(1)}, u32[]{:S(2)}, u32[]{:S(2)}) %all-to-all-start.1) | async-done | bytes 262176 | tf_op jit(solution)/shard_map/all_to_all | solution.py:657
  68.9 5.1 %analysis.1 = f32[16,24,128]{2,1,0:T(8,128)S(1)} custom-call(s32[1]{0:T(128)} %bitcast.place_ref, s32[512]{0:T(512)} %map_ref.5, f32[32,16,128]{2,1,0:T(8,128)S(1)} %all-to-all-done.1.v_ref, f32[32,512]{1,0:T(8,128)} %bitcast.25, f32[32,512]{1,0:T(8,128)} %bitcast.27, f32[2,512]{1,0:T(2,128)} %bitcast.30, f32[2,512]{1,0:T(2,128)} %get-tuple-element.31.diag_ref, ...), custom_call_target="tpu_custom_call" | custom-call | tf_op jit(solution)/shard_map/analysis/pallas_call | solution.py:554
  74.1 23.9 %all_to_all.20.x_ref = f32[16,24,128]{2,1,0:T(8,128)S(1)} all-to-all(f32[16,24,128]{2,1,0:T(8,128)S(1)} %analysis.1), channel_id=1, replica_groups=mesh['row'=16,'ma'=32] {'row'}, dimensions={0} | all-to-all | bytes 393216 | tf_op jit(solution)/shard_map/all_to_all | solution.py:664
  98.0 0.1 radial.1
  98.0 11.6 %all_to_all.21.x_ref = f32[16,16,128]{2,1,0:T(8,128)S(1)} all-to-all(f32[16,16,128]{2,1,0:T(8,128)S(1)} %radial.1), channel_id=1, replica_groups=mesh['row'=16,'ma'=32] {'row'}, dimensions={0} | all-to-all | bytes 262144 | tf_op jit(solution)/shard_map/all_to_all | solution.py:665
  109.7 0.8 assemble.1
  (4 shorter events, 0.0 us)
Async XLA Ops:
  0.6 17.6 %copy-start.1 = (s32[512]{0:T(512)S(1)}, s32[512]{0:T(512)}, u32[]{:S(2)}) copy-start(s32[512]{0:T(512)} %map_ref.5) | copy-start | bytes 6148
  7.6 29.9 %all-to-all-start = ((f32[32,48,128]{2,1,0:T(8,128)}), f32[32,48,128]{2,1,0:T(8,128)S(1)}, u32[]{:S(2)}, u32[]{:S(2)}) async-start(f32[32,48,128]{2,1,0:T(8,128)} %synthesis.1.after_ref), calls=%async_computation | async-start | bytes 1572864 | tf_op jit(solution)/shard_map/all_to_all | solution.py:645
  28.6 19.7 %copy-start = (f32[48,128]{1,0:T(8,128)S(1)}, f32[48,128]{1,0:T(8,128)}, u32[]{:S(2)}) copy-start(f32[48,128]{1,0:T(8,128)} %constant.50.clone.per_ref) | copy-start | bytes 73732
  37.5 12.4 %collective-permute-start = (f32[32,16,128]{2,1,0:T(8,128)S(1)}, f32[32,16,128]{2,1,0:T(8,128)S(1)}, u32[]{:S(2)}, u32[]{:S(2)}) collective-permute-start(f32[32,16,128]{2,1,0:T(8,128)S(1)} %slice.12), channel_id=1, source_target_pairs={{0,32},{32,0},{64,96},{96,64},{128,160},{160,128},{192,224},{224,1... | collective-permute-start | bytes 786440 | tf_op jit(solution)/shard_map/ppermute | solution.py:654
  44.3 7.9 %collective-permute-start.1 = (f32[32,16,128]{2,1,0:T(8,128)S(1)}, f32[32,16,128]{2,1,0:T(8,128)S(1)}, u32[]{:S(2)}, u32[]{:S(2)}) collective-permute-start(f32[32,16,128]{2,1,0:T(8,128)S(1)} %slice.12), channel_id=1, source_target_pairs={{32,64},{96,128},{160,192},{224,256},{288,320},{352,384},{416,448}... | collective-permute-start | bytes 786440 | tf_op jit(solution)/shard_map/ppermute | solution.py:653
  49.8 9.4 %copy-start.2 = (f32[2,1,512]{2,1,0:T(1,128)S(1)}, f32[2,1,512]{2,1,0:T(1,128)}, u32[]{:S(2)}) copy-start(f32[2,1,512]{2,1,0:T(1,128)} %param.16) | copy-start | bytes 12292
  49.8 10.0 %copy-start.3 = (f32[2,1,512]{2,1,0:T(1,128)S(1)}, f32[2,1,512]{2,1,0:T(1,128)}, u32[]{:S(2)}) copy-start(f32[2,1,512]{2,1,0:T(1,128)} %param.17) | copy-start | bytes 12292
  49.8 10.0 %copy-start.4 = (f32[2,1,512]{2,1,0:T(1,128)S(1)}, f32[2,1,512]{2,1,0:T(1,128)}, u32[]{:S(2)}) copy-start(f32[2,1,512]{2,1,0:T(1,128)} %param.18) | copy-start | bytes 12292
  54.7 14.2 %all-to-all-start.1 = ((f32[32,16,128]{2,1,0:T(8,128)}), f32[32,16,128]{2,1,0:T(8,128)S(1)}, u32[]{:S(2)}, u32[]{:S(2)}) async-start(f32[32,16,128]{2,1,0:T(8,128)} %forcing.1), calls=%async_computation.1 | async-start | bytes 524288 | tf_op jit(solution)/shard_map/all_to_all | solution.py:657

commit v3 on v2

--- a/solution.py
+++ b/solution.py
@@ -15,7 +15,7 @@
 QUARTER = NLON // 4
 GROUP = 16
 PAIRS = GROUP // 2
-UNROLL = 4
+UNROLL = 8
 SHELLS = 16
 INNER = 0.35
 SPAN = 0.65
@@ -315,7 +315,8 @@
     for pc in range(4):
         high, low = split(stage[pc, 0:rows, :])
         wave_high, wave_low = tables[pc]
-        waves.append(dot_nn(high, wave_high) + (dot_nn(low, wave_high) + dot_nn(high, wave_low)))
+        both = dot_nn(jnp.concatenate([high, low], axis=0), wave_high)
+        waves.append(both[:rows] + (both[rows:] + dot_nn(high, wave_low)))
     cos_even, sin_even, cos_odd, sin_odd = waves
     ce, se = cos_even + cos_odd, sin_even + sin_odd
     co, so = cos_even - cos_odd, sin_even - sin_odd
@@ -403,7 +404,8 @@
             pc = par * 2 + c
             high, low = split(sides[pc])
             wave_high, wave_low = tables[pc]
-            parts.append(dot_nt(wave_high, high) + (dot_nt(wave_high, low) + dot_nt(wave_low, high)))
+            both = dot_nt(wave_high, jnp.concatenate([high, low], axis=0))
+            parts.append(both[:, :48] + (both[:, 48:] + dot_nt(wave_low, high)))
         pair = jnp.concatenate(parts + [jnp.zeros((256, 32), f32)], axis=1)
         out_ref[:, par * 8 : par * 8 + 8, :] = pair.reshape(32, 8, 128)
 

time: 111 us -> 111 us (level)
  no operation moved by 1% of the time
where the time goes in v3:
time: 111 us
  blocking collectives  35.6 us (32%)
  starting transfers between devices  25.9 us (23%)
  Pallas kernels  23.9 us (22%)
  waiting for transfers between devices  19.7 us (18%)
  other arithmetic  3.39 us (3%)
  local copies, waits for them, and re-layouts  1.61 us (1%)
    all_to_all x1, blocking collectives, body(): right = lax.all_to_all(right, 'row', 0, 0, tiled=True)  23.9 us
    all_to_all x1, blocking collectives, body(): solved = lax.all_to_all(solve(right), 'row', 0, 0, tiled=True)  11.6 us
    all_to_all x1, starting transfers between devices, body(): chunk = lax.all_to_all(chunk, 'ma', 0, 0, tiled=True)  10.7 us
    all_to_all x1, waiting for transfers between devices, body(): chunk = lax.all_to_all(chunk, 'ma', 0, 0, tiled=True)  8.74 us
    all_to_all x1, waiting for transfers between devices, body(): spectra = lax.all_to_all(spectra, 'ma', 0, 0, tiled=True)  8.52 us
    pallas_call x1, Pallas kernels, synthesis(): pl.pallas_call(synthesis_kernel, in_specs=specs(2, 6), out_shape=near_out...  7.42 us
    ppermute x1, starting transfers between devices, body(): chip = lax.ppermute(profiles, 'row', near_pairs)  6.85 us
    pallas_call x1, Pallas kernels, tables(): pl.pallas_call(table_kernel, in_specs=specs(2, 2) + [pl.BlockSpec(memory_...  6.62 us
  transfers between devices with their start and end apart: 4, of which 3 were waited for; matrix products, arithmetic and copies ran while one was open for 4% of the time, Pallas kernels for 7%

profile of v3, /device:TPU:1, one launch (start us, length us, event | category | flops | bytes accessed | tf_op | source)
XLA Modules:
  0.0 110.8 jit_solution(6690908387955854401)
XLA Ops:
  0.6 0.0 copy-start.1
  0.6 7.4 %synthesis.1.after_ref = f32[32,48,128]{2,1,0:T(8,128)} custom-call(s32[1]{0:T(128)} %bitcast.place_ref, s32[512]{0:T(512)} %map_ref.5, f32[32,512]{1,0:T(8,128)} %bitcast.28, f32[32,512]{1,0:T(8,128)} %bitcast.24, f32[32,512]{1,0:T(8,128)} %bitcast.26, f32[32,512]{1,0:T(8,128)} %bitcast.29, f32[8,384]{1,0:T(8,128)} %constant.48.clone.lat_ref, ...), custom_call_target="tpu_custom_call" | custom-call | tf_op jit(solution)/shard_map/synthesis/pallas_call | solution.py:298
  8.1 10.7 %all-to-all-start = ((f32[32,48,128]{2,1,0:T(8,128)}), f32[32,48,128]{2,1,0:T(8,128)S(1)}, u32[]{:S(2)}, u32[]{:S(2)}) async-start(f32[32,48,128]{2,1,0:T(8,128)} %synthesis.1.after_ref), calls=%async_computation | async-start | bytes 1572864 | tf_op jit(solution)/shard_map/all_to_all | solution.py:647
  18.7 0.0 copy-done.1
  18.8 0.1 reshape.182
  18.9 6.6 %legendre.1 = (bf16[8,768,512]{2,1,0:T(8,128)(2,1)}, f32[8,384]{1,0:T(8,128)}) custom-call(s32[1]{0:T(128)} %bitcast.place_ref, s32[512]{0:T(512)} %map_ref.5, f32[8,384]{1,0:T(8,128)} %constant.48.clone.lat_ref, f32[8,512]{1,0:T(8,128)} %constant.49.clone.norm_ref, f32[32,48,128]{2,1,0:T(8,128)} %synthesis.1.after_ref), custom_call_target="tpu_custom_call" | custom-call | tf_op jit(solution)/shard_map/legendre/pallas_call | solution.py:445
  25.5 0.2 slice_reduce_fusion
  25.8 3.3 %fusion.4 = (f32[2,1,256,384]{3,2,1,0:T(8,128)S(1)}, f32[2,1,256,384]{3,2,1,0:T(8,128)S(1)}) fusion(s32[384]{0:T(512)S(1)} %multiply_add_fusion, s32[2,256]{1,0:T(2,128)S(1)} %get-tuple-element.29), kind=kLoop, calls=%fused_computation.8 | loop fusion | flops 1966080 | bytes 1576448 | tf_op jit(solution)/shard_map/cos | solution.py:623
  29.1 0.0 copy-start
  29.1 0.1 pad_maximum_fusion
  29.2 8.7 %all-to-all-done.x_ref = f32[32,48,128]{2,1,0:T(8,128)S(1)} async-done(((f32[32,48,128]{2,1,0:T(8,128)}), f32[32,48,128]{2,1,0:T(8,128)S(1)}, u32[]{:S(2)}, u32[]{:S(2)}) %all-to-all-start) | async-done | bytes 786464 | tf_op jit(solution)/shard_map/all_to_all | solution.py:647
  38.0 6.8 %collective-permute-start = (f32[32,16,128]{2,1,0:T(8,128)S(1)}, f32[32,16,128]{2,1,0:T(8,128)S(1)}, u32[]{:S(2)}, u32[]{:S(2)}) collective-permute-start(f32[32,16,128]{2,1,0:T(8,128)S(1)} %slice.12), channel_id=1, source_target_pairs={{0,32},{32,0},{64,96},{96,64},{128,160},{160,128},{192,224},{224,1... | collective-permute-start | bytes 786440 | tf_op jit(solution)/shard_map/ppermute | solution.py:656
  44.8 3.9 %collective-permute-start.1 = (f32[32,16,128]{2,1,0:T(8,128)S(1)}, f32[32,16,128]{2,1,0:T(8,128)S(1)}, u32[]{:S(2)}, u32[]{:S(2)}) collective-permute-start(f32[32,16,128]{2,1,0:T(8,128)S(1)} %slice.12), channel_id=1, source_target_pairs={{32,64},{96,128},{160,192},{224,256},{288,320},{352,384},{416,448}... | collective-permute-start | bytes 786440 | tf_op jit(solution)/shard_map/ppermute | solution.py:655
  48.7 0.0 copy-done
  48.7 1.5 %flow.1.flow_ref = f32[4,72,384]{2,1,0:T(8,128)S(1)} custom-call(s32[1]{0:T(128)} %bitcast.place_ref, s32[1]{0:T(128)} %bitcast.1.shell_ref, f32[32,48,128]{2,1,0:T(8,128)S(1)} %all-to-all-done.x_ref, f32[4,256,384]{2,1,0:T(8,128)S(1)} %bitcast.22, f32[2,256]{1,0:T(2,128)S(1)} %get-tuple-element.28.order_ref, f32[48,128]{1,0:T(8,128)S(1)} %copy-done), custom_call_target="tpu_custom_call" | custom-call | tf_op jit(solution)/shard_map/flow/pallas_call | solution.py:360
  50.3 0.0 copy-start.2
  50.3 0.0 copy-start.3
  50.3 0.0 copy-start.4
  50.3 0.0 collective-permute-done.chip_ref
  50.3 2.4 %collective-permute-done.1.link_ref = f32[32,16,128]{2,1,0:T(8,128)S(1)} collective-permute-done((f32[32,16,128]{2,1,0:T(8,128)S(1)}, f32[32,16,128]{2,1,0:T(8,128)S(1)}, u32[]{:S(2)}, u32[]{:S(2)}) %collective-permute-start.1) | collective-permute-done | bytes 262176 | tf_op jit(solution)/shard_map/ppermute | solution.py:655
  52.7 2.3 %forcing.1 = f32[32,16,128]{2,1,0:T(8,128)} custom-call(s32[1]{0:T(128)} %bitcast.1.shell_ref, f32[32,16,128]{2,1,0:T(8,128)S(1)} %collective-permute-done.chip_ref, f32[32,16,128]{2,1,0:T(8,128)S(1)} %collective-permute-done.1.link_ref, f32[4,256,384]{2,1,0:T(8,128)S(1)} %bitcast.23, f32[4,72,384]{2,1,0:T(8,128)S(1)} %flow.1.flow_ref), custom_call_target="tpu_custom_call" | custom-call | tf_op jit(solution)/shard_map/forcing/pallas_call | solution.py:414
  55.0 4.5 %all-to-all-start.1 = ((f32[32,16,128]{2,1,0:T(8,128)}), f32[32,16,128]{2,1,0:T(8,128)S(1)}, u32[]{:S(2)}, u32[]{:S(2)}) async-start(f32[32,16,128]{2,1,0:T(8,128)} %forcing.1), calls=%async_computation.1 | async-start | bytes 524288 | tf_op jit(solution)/shard_map/all_to_all | solution.py:659
  59.5 0.0 copy-done.2
  59.5 0.6 copy.23
  60.1 0.0 copy-done.3
  60.1 0.0 copy-done.4
  60.1 0.6 copy_bitcast_fusion
  60.7 8.5 %all-to-all-done.1.v_ref = f32[32,16,128]{2,1,0:T(8,128)S(1)} async-done(((f32[32,16,128]{2,1,0:T(8,128)}), f32[32,16,128]{2,1,0:T(8,128)S(1)}, u32[]{:S(2)}, u32[]{:S(2)}) %all-to-all-start.1) | async-done | bytes 262176 | tf_op jit(solution)/shard_map/all_to_all | solution.py:659
  69.3 5.1 %analysis.1 = f32[16,24,128]{2,1,0:T(8,128)S(1)} custom-call(s32[1]{0:T(128)} %bitcast.place_ref, s32[512]{0:T(512)} %map_ref.5, f32[32,16,128]{2,1,0:T(8,128)S(1)} %all-to-all-done.1.v_ref, f32[32,512]{1,0:T(8,128)} %bitcast.25, f32[32,512]{1,0:T(8,128)} %bitcast.27, f32[2,512]{1,0:T(2,128)} %bitcast.30, f32[2,512]{1,0:T(2,128)} %get-tuple-element.31.diag_ref, ...), custom_call_target="tpu_custom_call" | custom-call | tf_op jit(solution)/shard_map/analysis/pallas_call | solution.py:556
  74.4 23.9 %all_to_all.20.x_ref = f32[16,24,128]{2,1,0:T(8,128)S(1)} all-to-all(f32[16,24,128]{2,1,0:T(8,128)S(1)} %analysis.1), channel_id=1, replica_groups=mesh['row'=16,'ma'=32] {'row'}, dimensions={0} | all-to-all | bytes 393216 | tf_op jit(solution)/shard_map/all_to_all | solution.py:666
  98.3 0.1 radial.1
  98.4 11.6 %all_to_all.21.x_ref = f32[16,16,128]{2,1,0:T(8,128)S(1)} all-to-all(f32[16,16,128]{2,1,0:T(8,128)S(1)} %radial.1), channel_id=1, replica_groups=mesh['row'=16,'ma'=32] {'row'}, dimensions={0} | all-to-all | bytes 262144 | tf_op jit(solution)/shard_map/all_to_all | solution.py:667
  110.0 0.8 assemble.1
  (4 shorter events, 0.0 us)
Async XLA Ops:
  0.6 18.1 %copy-start.1 = (s32[512]{0:T(512)S(1)}, s32[512]{0:T(512)}, u32[]{:S(2)}) copy-start(s32[512]{0:T(512)} %map_ref.5) | copy-start | bytes 6148
  8.1 29.9 %all-to-all-start = ((f32[32,48,128]{2,1,0:T(8,128)}), f32[32,48,128]{2,1,0:T(8,128)S(1)}, u32[]{:S(2)}, u32[]{:S(2)}) async-start(f32[32,48,128]{2,1,0:T(8,128)} %synthesis.1.after_ref), calls=%async_computation | async-start | bytes 1572864 | tf_op jit(solution)/shard_map/all_to_all | solution.py:647
  29.1 19.6 %copy-start = (f32[48,128]{1,0:T(8,128)S(1)}, f32[48,128]{1,0:T(8,128)}, u32[]{:S(2)}) copy-start(f32[48,128]{1,0:T(8,128)} %constant.50.clone.per_ref) | copy-start | bytes 73732
  38.0 12.4 %collective-permute-start = (f32[32,16,128]{2,1,0:T(8,128)S(1)}, f32[32,16,128]{2,1,0:T(8,128)S(1)}, u32[]{:S(2)}, u32[]{:S(2)}) collective-permute-start(f32[32,16,128]{2,1,0:T(8,128)S(1)} %slice.12), channel_id=1, source_target_pairs={{0,32},{32,0},{64,96},{96,64},{128,160},{160,128},{192,224},{224,1... | collective-permute-start | bytes 786440 | tf_op jit(solution)/shard_map/ppermute | solution.py:656
  44.8 7.9 %collective-permute-start.1 = (f32[32,16,128]{2,1,0:T(8,128)S(1)}, f32[32,16,128]{2,1,0:T(8,128)S(1)}, u32[]{:S(2)}, u32[]{:S(2)}) collective-permute-start(f32[32,16,128]{2,1,0:T(8,128)S(1)} %slice.12), channel_id=1, source_target_pairs={{32,64},{96,128},{160,192},{224,256},{288,320},{352,384},{416,448}... | collective-permute-start | bytes 786440 | tf_op jit(solution)/shard_map/ppermute | solution.py:655
  50.3 9.2 %copy-start.2 = (f32[2,1,512]{2,1,0:T(1,128)S(1)}, f32[2,1,512]{2,1,0:T(1,128)}, u32[]{:S(2)}) copy-start(f32[2,1,512]{2,1,0:T(1,128)} %param.16) | copy-start | bytes 12292
  50.3 9.8 %copy-start.3 = (f32[2,1,512]{2,1,0:T(1,128)S(1)}, f32[2,1,512]{2,1,0:T(1,128)}, u32[]{:S(2)}) copy-start(f32[2,1,512]{2,1,0:T(1,128)} %param.17) | copy-start | bytes 12292
  50.3 9.8 %copy-start.4 = (f32[2,1,512]{2,1,0:T(1,128)S(1)}, f32[2,1,512]{2,1,0:T(1,128)}, u32[]{:S(2)}) copy-start(f32[2,1,512]{2,1,0:T(1,128)} %param.18) | copy-start | bytes 12292
  55.0 14.2 %all-to-all-start.1 = ((f32[32,16,128]{2,1,0:T(8,128)}), f32[32,16,128]{2,1,0:T(8,128)S(1)}, u32[]{:S(2)}, u32[]{:S(2)}) async-start(f32[32,16,128]{2,1,0:T(8,128)} %forcing.1), calls=%async_computation.1 | async-start | bytes 524288 | tf_op jit(solution)/shard_map/all_to_all | solution.py:659
